TPU v7x, 256 devices: a whole 4x4x8 slice. The times are simulated.
256 devices in a mesh: dp: 64 (over z, x, core), rep: 4 (over y).
Axes of the slice: x: 4, y: 4, z: 8, core: 2. Of those that a mesh axis runs over, the one named last changes fastest.
Arguments:
- ecg: bfloat16 [4, 327680], P('rep', 'dp'), may hold values from -6 to 6
- conv_first: bfloat16 [5, 256], replicated, may hold values from -2.5 to 2.5
- conv_second: bfloat16 [512, 256], replicated, may hold values from -0.25 to 0.25
- conv_third: bfloat16 [512, 256], replicated, may hold values from -0.25 to 0.25
- enc_gain: float32 [256], replicated, may hold values from 0.1 to 1.9
- ctx_weight: bfloat16 [2, 512, 256], replicated, may hold values from -0.25 to 0.25
- head_weight: bfloat16 [256, 12, 256], replicated, may hold values from -0.375 to 0.375
- sources: int32 [4, 512, 4, 2], P('rep', 'dp'), may hold values from 0 to 63, as said below
Outputs:
- target_grad: float32 [4, 16384, 256], P('rep', 'dp')
- head_grad: float32 [4, 256, 12, 256], P('rep')
Inputs may be any that keep to these rules, and one draw needn't show every extreme that they name: sources[r, i, s] = (o, b): o is the piece index along the recording, b a block of 128 rows of that piece's 256 positions. Among the 32 entries of one piece at most 2 name the same piece o, and in every draw one piece o is named exactly 2 times by every piece of its recording.
All inputs are finite; a program needn't handle non-finite values.
Results may differ from a plain program's by a relative error of at most 0.0085.
Values may be sent and summed in bfloat16 or wider, within the bound.
No kernel may reach another device: no remote copies, remote signals or barrier semaphores. Data moves between devices by JAX's collectives and lax.ppermute only.
A program may use at most 128 MiB of HBM per device.

v0:
```python
import math

import jax
import jax.numpy as jnp
from jax import lax
from jax.experimental import pallas as pl
from jax.experimental.pallas import tpu as pltpu
from jax.sharding import Mesh, PartitionSpec as P

BF = jnp.bfloat16
F32 = jnp.float32
Z_ORDER = (4, 3, -3, 2, -2, 1, -1, 0)
Z_BUNDLES = (8,)


def gelu_exact(values):
    return jax.nn.gelu(values, approximate=False)


def encode(piece, conv_first, conv_second, conv_third, enc_gain, ctx_weight):
    channels = conv_first.shape[1]
    positions = piece.shape[0] // 20
    frames = piece.reshape(4 * positions, 5)
    hidden_one = gelu_exact(jnp.dot(frames, conv_first, preferred_element_type=F32)).astype(BF)
    hidden_two = gelu_exact(
        jnp.dot(
            hidden_one.reshape(2 * positions, 2 * channels),
            conv_second,
            preferred_element_type=F32,
        )
    ).astype(BF)
    mixed = jnp.dot(
        hidden_two.reshape(positions, 2 * channels), conv_third, preferred_element_type=F32
    )
    average = jnp.mean(mixed, -1, keepdims=True)
    centred = mixed - average
    variance = jnp.mean(centred * centred, -1, keepdims=True)
    latent = (centred / jnp.sqrt(variance + 1e-05) * enc_gain).astype(BF)
    latent_wide = latent.astype(F32)
    target = (
        latent_wide / jnp.sqrt(jnp.sum(latent_wide * latent_wide, -1, keepdims=True) + 1e-06)
    ).astype(BF)
    context = latent
    for layer_index in range(ctx_weight.shape[0]):
        dilation = 2**layer_index
        before = jnp.concatenate(
            [jnp.zeros((dilation, channels), BF), context[: positions - dilation]], 0
        )
        joined = jnp.concatenate([context, before], 1)
        update = gelu_exact(jnp.dot(joined, ctx_weight[layer_index], preferred_element_type=F32))
        context = (context.astype(F32) + update).astype(BF)
    return (target, context)


def query_kernel(
    tgt_ref, ctx_ref, hw_ref, q_ref, t_ref, inv_ref, exp_ref, ten_ref, pad_s, *, groups
):
    positions, channels = tgt_ref.shape
    horizon = hw_ref.shape[0]
    rows = positions // groups
    pad_s[:positions] = tgt_ref[...].astype(F32)
    pad_s[positions:] = jnp.zeros((16, channels), F32)
    position = lax.broadcasted_iota(jnp.int32, (positions, 1), 0)

    unroll = math.gcd(horizon, 3)

    def step(k, ahead):
        pred = jnp.dot(ctx_ref[...], hw_ref[k], preferred_element_type=F32)
        inv = 1.0 / jnp.sqrt(jnp.sum(pred * pred, -1, keepdims=True) + 1e-06)
        query = (pred * inv).astype(BF)
        shifted = pad_s[ahead + 1 : ahead + 1 + positions]
        score = 10.0 * jnp.sum(query.astype(F32) * shifted, -1, keepdims=True)
        usable = jnp.where(position + k + 1 < positions, 10.0, 0.0)
        part = pl.ds(pl.multiple_of(k * rows, rows), rows)
        q_ref[:, part, :] = query.reshape(groups, rows, -1)
        t_ref[:, part, :] = shifted.astype(BF).reshape(groups, rows, -1)
        inv_ref[:, part, :] = inv.reshape(groups, rows, 1)
        exp_ref[:, part, :] = jnp.exp(score).reshape(groups, rows, 1)
        ten_ref[:, part, :] = usable.reshape(groups, rows, 1)

    def steps(i, carry):
        for j in range(unroll):
            step(i * unroll + j, j)
        pad_s[:positions] = pad_s[unroll : unroll + positions]
        return carry

    lax.fori_loop(0, horizon // unroll, steps, 0)


def score_kernel(
    where_ref, q_ref, t_ref, inv_ref, exp_ref, ten_ref, *rest, positions, per_group, bank_count
):
    banks = rest[:bank_count]
    keep_ref, send_ref, pg_ref, p_ref = rest[bank_count : bank_count + 4]
    nbuf, blocks_s, sems, out_sems = rest[bank_count + 4 :]
    groups = q_ref.shape[0]
    horizon = pg_ref.shape[0]
    rows = positions // groups
    entries = groups * per_group

    def start(e, carry):
        bank_id = where_ref[0, e]
        row = where_ref[1, e]
        for a in range(bank_count):

            @pl.when(bank_id == a)
            def _():
                pltpu.make_async_copy(banks[a].at[row], nbuf.at[e], sems.at[e]).start()

        return carry

    lax.fori_loop(0, entries, start, 0)
    blocks_s[...] = jnp.zeros(blocks_s.shape, BF)

    def group(g, carry):
        for s in range(per_group):
            e = g * per_group + s
            pltpu.make_async_copy(banks[0].at[0], nbuf.at[e], sems.at[e]).wait()
        queries = q_ref[g]
        negatives = nbuf[pl.ds(g * per_group, per_group)].reshape(per_group * 128, -1)
        negative = lax.dot_general(
            queries, negatives, (((1,), (1,)), ((), ())), preferred_element_type=F32
        )
        neg_exp = jnp.exp2((10.0 * math.log2(math.e)) * negative)
        pos_exp = exp_ref[g]
        over = ten_ref[g] / (pos_exp + jnp.sum(neg_exp, -1, keepdims=True))
        weight = (neg_exp * over).astype(BF)
        pos_weight = pos_exp * over - ten_ref[g]
        neg_part = jnp.dot(weight, negatives, preferred_element_type=F32)
        neg_grad = lax.dot_general(
            weight, queries, (((0,), (0,)), ((), ())), preferred_element_type=F32
        )
        for s in range(per_group):
            e = g * per_group + s
            place = where_ref[2, e]
            block = neg_grad[s * 128 : (s + 1) * 128]
            blocks_s[place] = (blocks_s[place].astype(F32) + block).astype(BF)

        unit = queries.astype(F32)
        query_grad = pos_weight * t_ref[g].astype(F32) + neg_part
        radial = jnp.sum(unit * query_grad, -1, keepdims=True)
        pred_grad = ((query_grad - unit * radial) * inv_ref[g]).astype(BF)
        pos_term = pos_weight * unit
        at = pl.ds(pl.multiple_of(g * rows, rows), rows)
        for k in range(horizon):
            pg_ref[k, at, :] = pred_grad[k * rows : (k + 1) * rows]
            p_ref[k, at, :] = pos_term[k * rows : (k + 1) * rows]
        return carry

    lax.fori_loop(0, groups, group, 0)
    half = blocks_s.shape[0] // 2
    sent = pltpu.make_async_copy(blocks_s.at[pl.ds(half, half)], send_ref, out_sems.at[0])
    kept = pltpu.make_async_copy(blocks_s.at[pl.ds(0, half)], keep_ref, out_sems.at[1])
    sent.start()
    kept.start()
    sent.wait()
    kept.wait()


def head_kernel(core_ref, ctx_ref, pg_ref, p_ref, hkeep_ref, hsend_ref, pos_ref, pad_s):
    core = core_ref[0]
    half = hkeep_ref.shape[0]

    def head(i, carry):
        for ref, base in ((hkeep_ref, core), (hsend_ref, 1 - core)):
            part = lax.dot_general(
                ctx_ref[...],
                pg_ref[base * half + i],
                (((0,), (0,)), ((), ())),
                preferred_element_type=F32,
            )
            ref[i] = part.astype(BF)
        return carry

    lax.fori_loop(0, half, head, 0)
    positions = pos_ref.shape[0]
    pad_s[...] = jnp.zeros(pad_s.shape, F32)
    for k in range(p_ref.shape[0]):
        at = slice(k + 1, k + 1 + positions)
        pad_s[at] = pad_s[at] + p_ref[k]
    pos_ref[...] = pad_s[:positions]


def make_queries(target, context, head_maps, groups):
    positions, channels = target.shape
    rows = head_maps.shape[0] * positions // groups
    vmem = pl.BlockSpec(memory_space=pltpu.VMEM)
    return pl.pallas_call(
        lambda *refs: query_kernel(*refs, groups=groups),
        out_shape=(
            jax.ShapeDtypeStruct((groups, rows, channels), BF),
            jax.ShapeDtypeStruct((groups, rows, channels), BF),
            jax.ShapeDtypeStruct((groups, rows, 1), F32),
            jax.ShapeDtypeStruct((groups, rows, 1), F32),
            jax.ShapeDtypeStruct((groups, rows, 1), F32),
        ),
        in_specs=[vmem] * 3,
        out_specs=(vmem,) * 5,
        scratch_shapes=[pltpu.VMEM((positions + 16, channels), F32)],
        name="queries",
    )(target, context, head_maps)


def score(where, made, banks, horizon, positions, per_group):
    groups, _, channels = made[0].shape
    blocks = 2 * (positions // 128) * banks[0].shape[0]
    vmem = pl.BlockSpec(memory_space=pltpu.VMEM)
    hbm = pl.BlockSpec(memory_space=pl.ANY)
    return pl.pallas_call(
        lambda *refs: score_kernel(
            *refs, positions=positions, per_group=per_group, bank_count=len(banks)
        ),
        out_shape=(
            jax.ShapeDtypeStruct((blocks, 128, channels), BF),
            jax.ShapeDtypeStruct((blocks, 128, channels), BF),
            jax.ShapeDtypeStruct((horizon, positions, channels), BF),
            jax.ShapeDtypeStruct((horizon, positions, channels), F32),
        ),
        in_specs=[pl.BlockSpec(memory_space=pltpu.SMEM)] + [vmem] * 5 + [hbm] * len(banks),
        out_specs=(hbm, hbm, vmem, vmem),
        scratch_shapes=[
            pltpu.VMEM((groups * per_group, 128, channels), BF),
            pltpu.VMEM((2 * blocks, 128, channels), BF),
            pltpu.SemaphoreType.DMA((groups * per_group,)),
            pltpu.SemaphoreType.DMA((2,)),
        ],
        name="score",
    )(where, *made, *banks)


def head_product(core, context, pred_grad, pos_terms):
    horizon, positions, channels = pred_grad.shape
    vmem = pl.BlockSpec(memory_space=pltpu.VMEM)
    half = jax.ShapeDtypeStruct((horizon // 2, channels, channels), BF)
    return pl.pallas_call(
        head_kernel,
        out_shape=(half, half, jax.ShapeDtypeStruct((positions, channels), F32)),
        in_specs=[pl.BlockSpec(memory_space=pltpu.SMEM), vmem, vmem, vmem],
        out_specs=(vmem, vmem, vmem),
        scratch_shapes=[pltpu.VMEM((positions + 16, channels), F32)],
        name="heads",
    )(core.reshape(1), context, pred_grad, pos_terms)


def shift(values, axis, by):
    size = lax.axis_size(axis)
    return lax.ppermute(values, axis, [(i, (i + by) % size) for i in range(size)])


def exchange(values, axis):
    return lax.all_to_all(values, axis, 0, 0, tiled=True)


def add(*terms):
    total = terms[0].astype(F32)
    for term in terms[1:]:
        total = total + term.astype(F32)
    return total


def gather_targets(target, made):
    z_size = lax.axis_size("z")
    row = exchange(jnp.broadcast_to(target[None], (z_size,) + target.shape), "z")
    left = shift(row, "x", 1)
    right = shift(row, "x", -1)
    left, right, *made = lax.optimization_barrier((left, right, *made))
    far_low = shift(left[:, :128], "x", 1)
    far_high = shift(right[:, 128:], "x", -1)
    mine = [row, left, right, far_low, far_high]
    return mine + [shift(v, "c", 1) for v in mine], made


def pair(values, axis, bit):
    size = lax.axis_size(axis)
    return lax.ppermute(values, axis, [(i, i ^ bit) for i in range(size)])


def pick(values, axis, at):
    return lax.dynamic_index_in_dim(values, at, axis, keepdims=False)


def join(mine, other, bit, axis):
    low = jnp.where(bit == 0, mine, other)
    high = jnp.where(bit == 0, other, mine)
    return jnp.stack([low, high], axis)


def after(values, other):
    zero = other[(0,) * (other.ndim - 1) + (slice(0, 1),)].astype(F32) * 0.0
    return (values.astype(F32) + zero.reshape(())).astype(values.dtype)


def exchange_back(keep, send, head_keep, head_send):
    x_id, core = lax.axis_index("x"), lax.axis_index("c")
    x_size, channels = lax.axis_size("x"), keep.shape[-1]
    received = shift(send, "c", 1)
    head = add(head_keep, shift(head_send, "c", 1)).astype(BF)
    starts = [sum(Z_BUNDLES[:i]) for i in range(len(Z_BUNDLES))]

    firsts, seconds, terms = [], [], []
    for first, count in zip(starts, Z_BUNDLES):
        span = slice(first, first + count)
        far_low = add(keep[2, span, :128], received[2, span, :128]).astype(BF)
        far_high = add(keep[2, span, 128:], received[2, span, 128:]).astype(BF)
        firsts.append([shift(far_low, "x", 1), shift(far_high, "x", -1)])
    for i, (first, count) in enumerate(zip(starts, Z_BUNDLES)):
        span = slice(first, first + count)
        low, high, keep, received = lax.optimization_barrier((*firsts[i], keep, received))
        ahead = add(keep[1, span], received[1, span])
        behind = add(keep[3, span], received[3, span])
        ahead = jnp.concatenate([add(ahead[:, :128], low), ahead[:, 128:]], 1).astype(BF)
        behind = jnp.concatenate([behind[:, :128], add(behind[:, 128:], high)], 1).astype(BF)
        seconds.append([shift(ahead, "x", 1), shift(behind, "x", -1)])
    for i, (first, count) in enumerate(zip(starts, Z_BUNDLES)):
        span = slice(first, first + count)
        sums = add(keep[0, span], received[0, span], *seconds[i])
        arrived = []
        for j in range(count):
            by = Z_ORDER[first + j]
            arrived.append(sums[j] if by == 0 else shift(sums[j].astype(BF), "z", by))
        terms.append(lax.optimization_barrier(tuple(arrived)))
    total = add(*(term for group in terms for term in group))

    head = head.reshape(x_size, -1, channels)
    shares = [pick(head, 0, x_id)]
    for by in (1, -1, 2):
        shares.append(shift(pick(head, 0, (x_id + by) % x_size), "x", by))
    head = add(*shares).astype(BF)
    head = add(head, pair(head, "z", 1)).astype(BF)
    head = after(head, firsts[-1][1])
    head = add(head, pair(head, "z", 2)).astype(BF)
    head = add(head, pair(head, "z", 4)).astype(BF)
    head = after(head, seconds[0][1])
    pieces = jnp.stack([head] + [shift(head, "x", by) for by in (1, 2, -1)])
    head = jnp.concatenate([pick(pieces, 0, (x_id - x) % x_size) for x in range(x_size)], 0)
    head = after(head.reshape(head_keep.shape), terms[-1][0])
    both = join(head, shift(head, "c", 1), core, 0)
    return total, both.reshape((2 * head_keep.shape[0],) + head_keep.shape[1:])


def local(ecg, conv_first, conv_second, conv_third, enc_gain, ctx_weight, head_weight, sources):
    z_size, x_size, c_size = (lax.axis_size(a) for a in ("z", "x", "c"))
    groups, per_group = sources.shape[1:3]
    z_id, x_id, c_id = (lax.axis_index(a) for a in ("z", "x", "c"))
    owner = sources[0, :, :, 0].reshape(-1)
    block = sources[0, :, :, 1].reshape(-1)
    owner_z = owner // (x_size * c_size)
    owner_x = (owner // c_size) % x_size
    other_core = (owner % c_size != c_id).astype(jnp.int32)
    dx = (owner_x - x_id) % x_size
    dz = (owner_z - z_id) % z_size
    bank = jnp.where(
        dx == 0, 0, jnp.where(dx == 3, 1, jnp.where(dx == 1, 2, 3 + block))
    ) + 5 * other_core
    bank_row = jnp.where(dx == 2, owner_z, 2 * owner_z + block)
    position = jnp.where(dz == 0, 7, jnp.where(dz == 4, 0, jnp.where(dz < 4, 7 - 2 * dz, 2 * dz - 8)))
    place = 2 * (dx * z_size + position) + block
    place = place + 2 * x_size * z_size * other_core
    where = jnp.stack([bank, bank_row, place]).astype(jnp.int32)

    target, context = encode(
        ecg.reshape(-1), conv_first, conv_second, conv_third, enc_gain, ctx_weight
    )
    positions, channels = target.shape
    horizon = head_weight.shape[1]
    made = make_queries(target, context, head_weight.transpose(1, 0, 2), groups)
    banks, made = gather_targets(target, made)
    banks = [v.reshape(-1, 128, channels) for v in banks]
    keep, send, pred_grad, pos_terms = score(where, made, banks, horizon, positions, per_group)
    head_keep, head_send, pos_grad = head_product(
        c_id.astype(jnp.int32), context, pred_grad, pos_terms
    )
    shape = (x_size, z_size, positions, channels)
    summed, heads = exchange_back(
        keep.reshape(shape), send.reshape(shape), head_keep, head_send
    )
    target_grad = ((pos_grad + summed) / horizon)[None]
    factor = math.sqrt(channels / (z_size * x_size * c_size * positions))
    head_grad = (heads.astype(F32) * factor).transpose(1, 0, 2)[None]
    return (target_grad, head_grad)


def solution(mesh):
    fine = Mesh(mesh.devices.reshape(8, 4, 2, -1), ("z", "x", "c", "rep"))
    dp = ("z", "x", "c")
    in_specs = (P("rep", dp), P(), P(), P(), P(), P(), P(), P("rep", dp, None, None))
    out_specs = (P("rep", dp, None), P("rep", None, None, None))
    return jax.shard_map(local, mesh=fine, in_specs=in_specs, out_specs=out_specs, check_vma=False)
```

profile of v0, /device:TPU:1, one launch (start us, length us, event | category | flops | bytes accessed | tf_op | source)
XLA Modules:
  0.0 206.5 jit_solution(7908699407390682809)
XLA Ops:
  1.9 3.1 %fusion.3 = bf16[1024,256]{1,0:T(8,128)(2,1)S(1)} fusion(bf16[1024,5]{1,0:T(8,128)(2,1)S(1)} %reshape_reshape.3, bf16[5,256]{1,0:T(8,128)(2,1)} %param.9), kind=kOutput, calls=%fused_computation.10 | convolution fusion | flops 19660800 | bytes 537088 | tf_op jit(solution)/shard_map/dot_general | solution.py:24
  7.7 36.0 %all_to_all.5 = bf16[8,256,256]{2,1,0:T(8,128)(2,1)S(1)} all-to-all(bf16[8,256,256]{2,1,0:T(8,128)(2,1)S(1)} %broadcast_in_dim.12), channel_id=1, replica_groups=mesh['z'=8,'x'=4,'c'=2,'rep'=4] {'z'}, dimensions={0} | all-to-all | bytes 2097152 | tf_op jit(solution)/shard_map/all_to_all | solution.py:251
  44.9 1.4 collective-permute-start.1
  47.2 1.4 fusion.38.refs_1_.ctx_ref
  48.5 7.7 %queries.1 = (bf16[8,384,256]{2,1,0:T(8,128)(2,1)}, bf16[8,384,256]{2,1,0:T(8,128)(2,1)}, f32[8,384,1]{2,1,0:T(8,128)}, f32[8,384,1]{2,1,0:T(8,128)}, f32[8,384,1]{2,1,0:T(8,128)}) custom-call(bf16[256,256]{1,0:T(8,128)(2,1)} %copy-done.5, bf16[256,256]{1,0:T(8,128)(2,1)} %fusion.38.refs_1_.ctx_ref, bf16[12,256,256]{2,1,0:T(8,128)(2,1)} %bitcast.113), custom_call_target="tpu_custom_call" | custom-call | tf_op jit(solution)/shard_map/queries/pallas_call | solution.py:188
  56.3 10.8 %collective-permute-done = bf16[8,256,256]{2,1,0:T(8,128)(2,1)S(1)} collective-permute-done((bf16[8,256,256]{2,1,0:T(8,128)(2,1)S(1)}, bf16[8,256,256]{2,1,0:T(8,128)(2,1)S(1)}, u32[]{:S(2)}, u32[]{:S(2)}) %collective-permute-start) | collective-permute-done | bytes 1048608 | tf_op jit(solution)/shard_map/ppermute | solution.py:247
  69.7 1.8 collective-permute-start.3
  71.6 4.0 %collective-permute-start.4 = (bf16[8,256,256]{2,1,0:T(8,128)(2,1)S(1)}, bf16[8,256,256]{2,1,0:T(8,128)(2,1)}, u32[]{:S(2)}, u32[]{:S(2)}) collective-permute-start(bf16[8,256,256]{2,1,0:T(8,128)(2,1)S(1)} %all_to_all.5), channel_id=1, source_target_pairs={{0,4},{4,0},{1,5},{5,1},{2,6},{6,2},{3,7},{7,3},{8,12},{12,8},{9,1... | collective-permute-start | bytes 3145736 | tf_op jit(solution)/shard_map/ppermute | solution.py:247
  76.4 3.2 %collective-permute-done.2.refs_9_ = bf16[8,128,256]{2,1,0:T(8,128)(2,1)} collective-permute-done((bf16[8,128,256]{2,1,0:T(8,128)(2,1)}, bf16[8,128,256]{2,1,0:T(8,128)(2,1)}, u32[]{:S(2)}, u32[]{:S(2)}) %collective-permute-start.2) | collective-permute-done | bytes 524320 | tf_op jit(solution)/shard_map/ppermute | solution.py:247
  79.6 4.3 %collective-permute-start.7 = (bf16[8,128,256]{2,1,0:T(8,128)(2,1)}, bf16[8,128,256]{2,1,0:T(8,128)(2,1)S(1)}, u32[]{:S(2)}, u32[]{:S(2)}) collective-permute-start(bf16[8,128,256]{2,1,0:T(8,128)(2,1)} %collective-permute-done.2.refs_9_), channel_id=1, source_target_pairs={{0,4},{4,0},{1,5},{5,1},{2,6},{6,2},{3,7},{7,3},{8,12},{12,8},{9,1... | collective-permute-start | bytes 1572872 | tf_op jit(solution)/shard_map/ppermute | solution.py:247
  87.2 18.8 %score.1 = (bf16[64,128,256]{2,1,0:T(8,128)(2,1)}, bf16[64,128,256]{2,1,0:T(8,128)(2,1)}, bf16[12,256,256]{2,1,0:T(8,128)(2,1)}, f32[12,256,256]{2,1,0:T(8,128)}) custom-call(s32[3,32]{1,0:T(4,128)} %pad_add_fusion.refs_0_, bf16[8,384,256]{2,1,0:T(8,128)(2,1)} %get-tuple-element.38.refs_1_, bf16[8,384,256]{2,1,0:T(8,128)(2,1)} %get-tuple-element.39.refs_2_, ...), custom_call_target="tpu_custom_call" | custom-call | tf_op jit(solution)/shard_map/score/pallas_call | solution.py:209
  106.5 5.2 %heads.1 = (bf16[6,256,256]{2,1,0:T(8,128)(2,1)}, bf16[6,256,256]{2,1,0:T(8,128)(2,1)}, f32[256,256]{1,0:T(8,128)}) custom-call(s32[1]{0:T(128)} %bitcast.core_ref, bf16[256,256]{1,0:T(8,128)(2,1)} %fusion.38.refs_1_.ctx_ref, bf16[12,256,256]{2,1,0:T(8,128)(2,1)} %get-tuple-element.45.pg_ref, f32[12,256,256]{2,1,0:T(8,128)} %get-tuple-element.46.p_ref), custom_call_target="tpu_custom_call" | custom-call | tf_op jit(solution)/shard_map/heads/pallas_call | solution.py:235
  111.9 1.7 collective-permute-done.9
  113.6 2.6 %fusion.17 = (bf16[8,128,256]{2,1,0:T(8,128)(2,1)}, bf16[8,128,256]{2,1,0:T(8,128)(2,1)S(1)}) fusion(bf16[4,8,256,256]{3,2,1,0:T(8,128)(2,1)} %collective-permute-done.9, bf16[4,8,256,256]{3,2,1,0:T(8,128)(2,1)} %bitcast.103), kind=kLoop, calls=%fused_computation.44 | loop fusion | flops 2097152 | bytes 3145728 | tf_op jit(solution)/shard_map/convert_element_type | solution.py:304
  116.2 2.8 %collective-permute-start.11 = (bf16[8,128,256]{2,1,0:T(8,128)(2,1)}, bf16[8,128,256]{2,1,0:T(8,128)(2,1)S(1)}, u32[]{:S(2)}, u32[]{:S(2)}) collective-permute-start(bf16[8,128,256]{2,1,0:T(8,128)(2,1)} %get-tuple-element.74), channel_id=1, source_target_pairs={{0,24},{8,0},{16,8},{24,16},{1,25},{9,1},{17,9},{25,17},{2,26},{10... | collective-permute-start | bytes 1572872 | tf_op jit(solution)/shard_map/ppermute | solution.py:247
  119.4 2.7 %collective-permute-start.23 = (bf16[384,256]{1,0:T(8,128)(2,1)S(1)}, bf16[384,256]{1,0:T(8,128)(2,1)S(1)}, u32[]{:S(2)}, u32[]{:S(2)}) collective-permute-start(bf16[384,256]{1,0:T(8,128)(2,1)S(1)} %get-tuple-element.91), channel_id=1, source_target_pairs={{0,24},{8,0},{16,8},{24,16},{1,25},{9,1},{17,9},{25,17},{2,26},{10... | collective-permute-start | bytes 589832 | tf_op jit(solution)/shard_map/ppermute | solution.py:247
  123.2 7.1 %collective-permute-done.11 = bf16[8,128,256]{2,1,0:T(8,128)(2,1)S(1)} collective-permute-done((bf16[8,128,256]{2,1,0:T(8,128)(2,1)}, bf16[8,128,256]{2,1,0:T(8,128)(2,1)S(1)}, u32[]{:S(2)}, u32[]{:S(2)}) %collective-permute-start.11) | collective-permute-done | bytes 524320 | tf_op jit(solution)/shard_map/ppermute | solution.py:247
  130.3 2.8 %collective-permute-done.10 = bf16[8,128,256]{2,1,0:T(8,128)(2,1)S(1)} collective-permute-done((bf16[8,128,256]{2,1,0:T(8,128)(2,1)S(1)}, bf16[8,128,256]{2,1,0:T(8,128)(2,1)S(1)}, u32[]{:S(2)}, u32[]{:S(2)}) %collective-permute-start.10) | collective-permute-done | bytes 524320 | tf_op jit(solution)/shard_map/ppermute | solution.py:247
  133.1 2.9 %add_bitcast_fusion.1 = (f32[8,256,256]{2,1,0:T(8,128)S(1)}, f32[8,256,256]{2,1,0:T(8,128)S(1)}) fusion(bf16[4,8,256,256]{3,2,1,0:T(8,128)(2,1)} %collective-permute-done.9, bf16[4,8,256,256]{3,2,1,0:T(8,128)(2,1)} %bitcast.104), kind=kLoop, calls=%fused_computation.4 | loop fusion | flops 3145728 | bytes 8388608 | tf_op jit(solution)/shard_map/add | solution.py:257
  139.1 2.4 %collective-permute-done.22 = bf16[384,256]{1,0:T(8,128)(2,1)S(1)} collective-permute-done((bf16[384,256]{1,0:T(8,128)(2,1)S(1)}, bf16[384,256]{1,0:T(8,128)(2,1)S(1)}, u32[]{:S(2)}, u32[]{:S(2)}) %collective-permute-start.22) | collective-permute-done | bytes 196640 | tf_op jit(solution)/shard_map/ppermute | solution.py:247
  143.7 3.1 %collective-permute-done.25 = bf16[384,256]{1,0:T(8,128)(2,1)S(1)} collective-permute-done((bf16[384,256]{1,0:T(8,128)(2,1)S(1)}, bf16[384,256]{1,0:T(8,128)(2,1)S(1)}, u32[]{:S(2)}, u32[]{:S(2)}) %collective-permute-start.25) | collective-permute-done | bytes 196640 | tf_op jit(solution)/shard_map/ppermute | solution.py:275
  148.0 11.2 %collective-permute-done.26 = bf16[384,256]{1,0:T(8,128)(2,1)} collective-permute-done((bf16[384,256]{1,0:T(8,128)(2,1)}, bf16[384,256]{1,0:T(8,128)(2,1)}, u32[]{:S(2)}, u32[]{:S(2)}) %collective-permute-start.26) | collective-permute-done | bytes 196640 | tf_op jit(solution)/shard_map/ppermute | solution.py:275
  160.2 2.6 %collective-permute-start.27 = (bf16[384,256]{1,0:T(8,128)(2,1)S(1)}, bf16[384,256]{1,0:T(8,128)(2,1)S(1)}, u32[]{:S(2)}, u32[]{:S(2)}) collective-permute-start(bf16[384,256]{1,0:T(8,128)(2,1)S(1)} %add_convert_fusion.6), channel_id=1, source_target_pairs={{0,128},{32,160},{64,192},{96,224},{128,0},{160,32},{192,64},{224,... | collective-permute-start | bytes 589832 | tf_op jit(solution)/shard_map/ppermute | solution.py:275
  164.1 2.1 fusion.92
  166.2 2.9 %collective-permute-start.14 = (bf16[256,256]{1,0:T(8,128)(2,1)S(1)}, bf16[256,256]{1,0:T(8,128)(2,1)S(1)}, u32[]{:S(2)}, u32[]{:S(2)}) collective-permute-start(bf16[256,256]{1,0:T(8,128)(2,1)S(1)} %get-tuple-element.84), channel_id=1, source_target_pairs={{0,128},{32,160},{64,192},{96,224},{128,0},{160,32},{192,64},{224,... | collective-permute-start | bytes 393224 | tf_op jit(solution)/shard_map/ppermute | solution.py:247
  170.5 3.1 %collective-permute-start.16 = (bf16[256,256]{1,0:T(8,128)(2,1)S(1)}, bf16[256,256]{1,0:T(8,128)(2,1)S(1)}, u32[]{:S(2)}, u32[]{:S(2)}) collective-permute-start(bf16[256,256]{1,0:T(8,128)(2,1)S(1)} %get-tuple-element.82), channel_id=1, source_target_pairs={{0,160},{32,192},{64,224},{96,0},{128,32},{160,64},{192,96},{224,1... | collective-permute-start | bytes 393224 | tf_op jit(solution)/shard_map/ppermute | solution.py:247
  174.8 2.3 %collective-permute-start.18 = (bf16[256,256]{1,0:T(8,128)(2,1)S(1)}, bf16[256,256]{1,0:T(8,128)(2,1)S(1)}, u32[]{:S(2)}, u32[]{:S(2)}) collective-permute-start(bf16[256,256]{1,0:T(8,128)(2,1)S(1)} %get-tuple-element.80), channel_id=1, source_target_pairs={{0,192},{32,224},{64,0},{96,32},{128,64},{160,96},{192,128},{224,1... | collective-permute-start | bytes 393224 | tf_op jit(solution)/shard_map/ppermute | solution.py:247
  178.5 12.9 %collective-permute-done.15 = bf16[256,256]{1,0:T(8,128)(2,1)S(1)} collective-permute-done((bf16[256,256]{1,0:T(8,128)(2,1)S(1)}, bf16[256,256]{1,0:T(8,128)(2,1)S(1)}, u32[]{:S(2)}, u32[]{:S(2)}) %collective-permute-start.15) | collective-permute-done | bytes 131104 | tf_op jit(solution)/shard_map/ppermute | solution.py:247
  192.8 2.2 %collective-permute-start.19 = (bf16[256,256]{1,0:T(8,128)(2,1)S(1)}, bf16[256,256]{1,0:T(8,128)(2,1)S(1)}, u32[]{:S(2)}, u32[]{:S(2)}) collective-permute-start(bf16[256,256]{1,0:T(8,128)(2,1)S(1)} %get-tuple-element.79), channel_id=1, source_target_pairs={{0,32},{32,64},{64,96},{96,128},{128,160},{160,192},{192,224},{224... | collective-permute-start | bytes 393224 | tf_op jit(solution)/shard_map/ppermute | solution.py:247
  195.6 2.6 %collective-permute-done.19 = bf16[256,256]{1,0:T(8,128)(2,1)S(1)} collective-permute-done((bf16[256,256]{1,0:T(8,128)(2,1)S(1)}, bf16[256,256]{1,0:T(8,128)(2,1)S(1)}, u32[]{:S(2)}, u32[]{:S(2)}) %collective-permute-start.19) | collective-permute-done | bytes 131104 | tf_op jit(solution)/shard_map/ppermute | solution.py:247
  200.8 1.7 collective-permute-start.31
  204.6 2.0 convert_multiply_fusion
  (124 shorter events, 32.1 us)
Async XLA Ops:
  43.7 23.4 %collective-permute-start = (bf16[8,256,256]{2,1,0:T(8,128)(2,1)S(1)}, bf16[8,256,256]{2,1,0:T(8,128)(2,1)S(1)}, u32[]{:S(2)}, u32[]{:S(2)}) collective-permute-start(bf16[8,256,256]{2,1,0:T(8,128)(2,1)S(1)} %all_to_all.5), channel_id=1, source_target_pairs={{0,8},{8,16},{16,24},{24,0},{1,9},{9,17},{17,25},{25,1},{2,10},{10... | collective-permute-start | bytes 3145736 | tf_op jit(solution)/shard_map/ppermute | solution.py:247
  44.9 22.2 %collective-permute-start.1 = (bf16[8,256,256]{2,1,0:T(8,128)(2,1)S(1)}, bf16[8,256,256]{2,1,0:T(8,128)(2,1)S(1)}, u32[]{:S(2)}, u32[]{:S(2)}) collective-permute-start(bf16[8,256,256]{2,1,0:T(8,128)(2,1)S(1)} %all_to_all.5), channel_id=1, source_target_pairs={{0,24},{8,0},{16,8},{24,16},{1,25},{9,1},{17,9},{25,17},{2,26},{10... | collective-permute-start | bytes 3145736 | tf_op jit(solution)/shard_map/ppermute | solution.py:247
  68.0 11.5 %collective-permute-start.2 = (bf16[8,128,256]{2,1,0:T(8,128)(2,1)}, bf16[8,128,256]{2,1,0:T(8,128)(2,1)}, u32[]{:S(2)}, u32[]{:S(2)}) collective-permute-start(bf16[8,128,256]{2,1,0:T(8,128)(2,1)} %slice.114), channel_id=1, source_target_pairs={{0,8},{8,16},{16,24},{24,0},{1,9},{9,17},{17,25},{25,1},{2,10},{10... | collective-permute-start | bytes 1572872 | tf_op jit(solution)/shard_map/ppermute | solution.py:247
  69.7 14.2 %collective-permute-start.3 = (bf16[8,128,256]{2,1,0:T(8,128)(2,1)}, bf16[8,128,256]{2,1,0:T(8,128)(2,1)}, u32[]{:S(2)}, u32[]{:S(2)}) collective-permute-start(bf16[8,128,256]{2,1,0:T(8,128)(2,1)} %slice.115), channel_id=1, source_target_pairs={{0,24},{8,0},{16,8},{24,16},{1,25},{9,1},{17,9},{25,17},{2,26},{10... | collective-permute-start | bytes 1572872 | tf_op jit(solution)/shard_map/ppermute | solution.py:247
  71.6 13.5 %collective-permute-start.4 = (bf16[8,256,256]{2,1,0:T(8,128)(2,1)S(1)}, bf16[8,256,256]{2,1,0:T(8,128)(2,1)}, u32[]{:S(2)}, u32[]{:S(2)}) collective-permute-start(bf16[8,256,256]{2,1,0:T(8,128)(2,1)S(1)} %all_to_all.5), channel_id=1, source_target_pairs={{0,4},{4,0},{1,5},{5,1},{2,6},{6,2},{3,7},{7,3},{8,12},{12,8},{9,1... | collective-permute-start | bytes 3145736 | tf_op jit(solution)/shard_map/ppermute | solution.py:247
  75.5 10.9 %collective-permute-start.5 = (bf16[8,256,256]{2,1,0:T(8,128)(2,1)S(1)}, bf16[8,256,256]{2,1,0:T(8,128)(2,1)}, u32[]{:S(2)}, u32[]{:S(2)}) collective-permute-start(bf16[8,256,256]{2,1,0:T(8,128)(2,1)S(1)} %collective-permute-done), channel_id=1, source_target_pairs={{0,4},{4,0},{1,5},{5,1},{2,6},{6,2},{3,7},{7,3},{8,12},{12,8},{9,1... | collective-permute-start | bytes 3145736 | tf_op jit(solution)/shard_map/ppermute | solution.py:247
  75.5 10.9 %collective-permute-start.6 = (bf16[8,256,256]{2,1,0:T(8,128)(2,1)S(1)}, bf16[8,256,256]{2,1,0:T(8,128)(2,1)}, u32[]{:S(2)}, u32[]{:S(2)}) collective-permute-start(bf16[8,256,256]{2,1,0:T(8,128)(2,1)S(1)} %collective-permute-done.1), channel_id=1, source_target_pairs={{0,4},{4,0},{1,5},{5,1},{2,6},{6,2},{3,7},{7,3},{8,12},{12,8},{9,1... | collective-permute-start | bytes 3145736 | tf_op jit(solution)/shard_map/ppermute | solution.py:247
  79.6 6.1 %collective-permute-start.7 = (bf16[8,128,256]{2,1,0:T(8,128)(2,1)}, bf16[8,128,256]{2,1,0:T(8,128)(2,1)S(1)}, u32[]{:S(2)}, u32[]{:S(2)}) collective-permute-start(bf16[8,128,256]{2,1,0:T(8,128)(2,1)} %collective-permute-done.2.refs_9_), channel_id=1, source_target_pairs={{0,4},{4,0},{1,5},{5,1},{2,6},{6,2},{3,7},{7,3},{8,12},{12,8},{9,1... | collective-permute-start | bytes 1572872 | tf_op jit(solution)/shard_map/ppermute | solution.py:247
  83.9 2.5 %collective-permute-start.8 = (bf16[8,128,256]{2,1,0:T(8,128)(2,1)}, bf16[8,128,256]{2,1,0:T(8,128)(2,1)S(1)}, u32[]{:S(2)}, u32[]{:S(2)}) collective-permute-start(bf16[8,128,256]{2,1,0:T(8,128)(2,1)} %collective-permute-done.3.refs_10_), channel_id=1, source_target_pairs={{0,4},{4,0},{1,5},{5,1},{2,6},{6,2},{3,7},{7,3},{8,12},{12,8},{9,1... | collective-permute-start | bytes 1572872 | tf_op jit(solution)/shard_map/ppermute | solution.py:247
  106.0 7.6 %collective-permute-start.9 = (bf16[4,8,256,256]{3,2,1,0:T(8,128)(2,1)}, bf16[4,8,256,256]{3,2,1,0:T(8,128)(2,1)}, u32[]{:S(2)}, u32[]{:S(2)}) collective-permute-start(bf16[4,8,256,256]{3,2,1,0:T(8,128)(2,1)} %bitcast.119), channel_id=1, source_target_pairs={{0,4},{4,0},{1,5},{5,1},{2,6},{6,2},{3,7},{7,3},{8,12},{12,8},{9,1... | collective-permute-start | bytes 12582920 | tf_op jit(solution)/shard_map/ppermute | solution.py:247
  111.7 7.3 %collective-permute-start.21 = (bf16[6,256,256]{2,1,0:T(8,128)(2,1)}, bf16[6,256,256]{2,1,0:T(8,128)(2,1)S(1)}, u32[]{:S(2)}, u32[]{:S(2)}) collective-permute-start(bf16[6,256,256]{2,1,0:T(8,128)(2,1)} %get-tuple-element.63), channel_id=1, source_target_pairs={{0,4},{4,0},{1,5},{5,1},{2,6},{6,2},{3,7},{7,3},{8,12},{12,8},{9,1... | collective-permute-start | bytes 2359304 | tf_op jit(solution)/shard_map/ppermute | solution.py:247
  116.2 14.0 %collective-permute-start.11 = (bf16[8,128,256]{2,1,0:T(8,128)(2,1)}, bf16[8,128,256]{2,1,0:T(8,128)(2,1)S(1)}, u32[]{:S(2)}, u32[]{:S(2)}) collective-permute-start(bf16[8,128,256]{2,1,0:T(8,128)(2,1)} %get-tuple-element.74), channel_id=1, source_target_pairs={{0,24},{8,0},{16,8},{24,16},{1,25},{9,1},{17,9},{25,17},{2,26},{10... | collective-permute-start | bytes 1572872 | tf_op jit(solution)/shard_map/ppermute | solution.py:247
  119.0 14.0 %collective-permute-start.10 = (bf16[8,128,256]{2,1,0:T(8,128)(2,1)S(1)}, bf16[8,128,256]{2,1,0:T(8,128)(2,1)S(1)}, u32[]{:S(2)}, u32[]{:S(2)}) collective-permute-start(bf16[8,128,256]{2,1,0:T(8,128)(2,1)S(1)} %get-tuple-element.75), channel_id=1, source_target_pairs={{0,8},{8,16},{16,24},{24,0},{1,9},{9,17},{17,25},{25,1},{2,10},{10... | collective-permute-start | bytes 1572872 | tf_op jit(solution)/shard_map/ppermute | solution.py:247
  119.3 22.2 %collective-permute-start.22 = (bf16[384,256]{1,0:T(8,128)(2,1)S(1)}, bf16[384,256]{1,0:T(8,128)(2,1)S(1)}, u32[]{:S(2)}, u32[]{:S(2)}) collective-permute-start(bf16[384,256]{1,0:T(8,128)(2,1)S(1)} %get-tuple-element.89), channel_id=1, source_target_pairs={{0,8},{8,16},{16,24},{24,0},{1,9},{9,17},{17,25},{25,1},{2,10},{10... | collective-permute-start | bytes 589832 | tf_op jit(solution)/shard_map/ppermute | solution.py:247
  119.4 22.1 %collective-permute-start.23 = (bf16[384,256]{1,0:T(8,128)(2,1)S(1)}, bf16[384,256]{1,0:T(8,128)(2,1)S(1)}, u32[]{:S(2)}, u32[]{:S(2)}) collective-permute-start(bf16[384,256]{1,0:T(8,128)(2,1)S(1)} %get-tuple-element.91), channel_id=1, source_target_pairs={{0,24},{8,0},{16,8},{24,16},{1,25},{9,1},{17,9},{25,17},{2,26},{10... | collective-permute-start | bytes 589832 | tf_op jit(solution)/shard_map/ppermute | solution.py:247
  122.1 19.4 %collective-permute-start.24 = (bf16[384,256]{1,0:T(8,128)(2,1)S(1)}, bf16[384,256]{1,0:T(8,128)(2,1)S(1)}, u32[]{:S(2)}, u32[]{:S(2)}) collective-permute-start(bf16[384,256]{1,0:T(8,128)(2,1)S(1)} %get-tuple-element.90), channel_id=1, source_target_pairs={{0,16},{8,24},{16,0},{24,8},{1,17},{9,25},{17,1},{25,9},{2,18},{10... | collective-permute-start | bytes 589832 | tf_op jit(solution)/shard_map/ppermute | solution.py:247
  136.3 26.6 %collective-permute-start.13 = (bf16[8,256,256]{2,1,0:T(8,128)(2,1)S(1)}, bf16[8,256,256]{2,1,0:T(8,128)(2,1)S(1)}, u32[]{:S(2)}, u32[]{:S(2)}) collective-permute-start(bf16[8,256,256]{2,1,0:T(8,128)(2,1)S(1)} %pad_maximum_fusion.1), channel_id=1, source_target_pairs={{0,24},{8,0},{16,8},{24,16},{1,25},{9,1},{17,9},{25,17},{2,26},{10... | collective-permute-start | bytes 3145736 | tf_op jit(solution)/shard_map/ppermute | solution.py:247
  138.4 25.7 %collective-permute-start.12 = (bf16[8,256,256]{2,1,0:T(8,128)(2,1)}, bf16[8,256,256]{2,1,0:T(8,128)(2,1)S(1)}, u32[]{:S(2)}, u32[]{:S(2)}) collective-permute-start(bf16[8,256,256]{2,1,0:T(8,128)(2,1)} %pad_maximum_fusion), channel_id=1, source_target_pairs={{0,8},{8,16},{16,24},{24,0},{1,9},{9,17},{17,25},{25,1},{2,10},{10... | collective-permute-start | bytes 3145736 | tf_op jit(solution)/shard_map/ppermute | solution.py:247
  141.6 5.2 %collective-permute-start.25 = (bf16[384,256]{1,0:T(8,128)(2,1)S(1)}, bf16[384,256]{1,0:T(8,128)(2,1)S(1)}, u32[]{:S(2)}, u32[]{:S(2)}) collective-permute-start(bf16[384,256]{1,0:T(8,128)(2,1)S(1)} %fusion.29), channel_id=1, source_target_pairs={{0,32},{32,0},{64,96},{96,64},{128,160},{160,128},{192,224},{224,1... | collective-permute-start | bytes 589832 | tf_op jit(solution)/shard_map/ppermute | solution.py:275
  147.5 11.6 %collective-permute-start.26 = (bf16[384,256]{1,0:T(8,128)(2,1)}, bf16[384,256]{1,0:T(8,128)(2,1)}, u32[]{:S(2)}, u32[]{:S(2)}) collective-permute-start(bf16[384,256]{1,0:T(8,128)(2,1)} %add_convert_fusion.7), channel_id=1, source_target_pairs={{0,64},{32,96},{64,0},{96,32},{128,192},{160,224},{192,128},{224,1... | collective-permute-start | bytes 589832 | tf_op jit(solution)/shard_map/ppermute | solution.py:275
  160.2 14.6 %collective-permute-start.27 = (bf16[384,256]{1,0:T(8,128)(2,1)S(1)}, bf16[384,256]{1,0:T(8,128)(2,1)S(1)}, u32[]{:S(2)}, u32[]{:S(2)}) collective-permute-start(bf16[384,256]{1,0:T(8,128)(2,1)S(1)} %add_convert_fusion.6), channel_id=1, source_target_pairs={{0,128},{32,160},{64,192},{96,224},{128,0},{160,32},{192,64},{224,... | collective-permute-start | bytes 589832 | tf_op jit(solution)/shard_map/ppermute | solution.py:275
  166.2 12.3 %collective-permute-start.14 = (bf16[256,256]{1,0:T(8,128)(2,1)S(1)}, bf16[256,256]{1,0:T(8,128)(2,1)S(1)}, u32[]{:S(2)}, u32[]{:S(2)}) collective-permute-start(bf16[256,256]{1,0:T(8,128)(2,1)S(1)} %get-tuple-element.84), channel_id=1, source_target_pairs={{0,128},{32,160},{64,192},{96,224},{128,0},{160,32},{192,64},{224,... | collective-permute-start | bytes 393224 | tf_op jit(solution)/shard_map/ppermute | solution.py:247
  169.1 22.3 %collective-permute-start.15 = (bf16[256,256]{1,0:T(8,128)(2,1)S(1)}, bf16[256,256]{1,0:T(8,128)(2,1)S(1)}, u32[]{:S(2)}, u32[]{:S(2)}) collective-permute-start(bf16[256,256]{1,0:T(8,128)(2,1)S(1)} %get-tuple-element.83), channel_id=1, source_target_pairs={{0,96},{32,128},{64,160},{96,192},{128,224},{160,0},{192,32},{224,... | collective-permute-start | bytes 393224 | tf_op jit(solution)/shard_map/ppermute | solution.py:247
  170.5 22.3 %collective-permute-start.16 = (bf16[256,256]{1,0:T(8,128)(2,1)S(1)}, bf16[256,256]{1,0:T(8,128)(2,1)S(1)}, u32[]{:S(2)}, u32[]{:S(2)}) collective-permute-start(bf16[256,256]{1,0:T(8,128)(2,1)S(1)} %get-tuple-element.82), channel_id=1, source_target_pairs={{0,160},{32,192},{64,224},{96,0},{128,32},{160,64},{192,96},{224,1... | collective-permute-start | bytes 393224 | tf_op jit(solution)/shard_map/ppermute | solution.py:247
  173.6 19.2 %collective-permute-start.17 = (bf16[256,256]{1,0:T(8,128)(2,1)S(1)}, bf16[256,256]{1,0:T(8,128)(2,1)S(1)}, u32[]{:S(2)}, u32[]{:S(2)}) collective-permute-start(bf16[256,256]{1,0:T(8,128)(2,1)S(1)} %get-tuple-element.81), channel_id=1, source_target_pairs={{0,64},{32,96},{64,128},{96,160},{128,192},{160,224},{192,0},{224,... | collective-permute-start | bytes 393224 | tf_op jit(solution)/shard_map/ppermute | solution.py:247
  174.8 20.1 %collective-permute-start.18 = (bf16[256,256]{1,0:T(8,128)(2,1)S(1)}, bf16[256,256]{1,0:T(8,128)(2,1)S(1)}, u32[]{:S(2)}, u32[]{:S(2)}) collective-permute-start(bf16[256,256]{1,0:T(8,128)(2,1)S(1)} %get-tuple-element.80), channel_id=1, source_target_pairs={{0,192},{32,224},{64,0},{96,32},{128,64},{160,96},{192,128},{224,1... | collective-permute-start | bytes 393224 | tf_op jit(solution)/shard_map/ppermute | solution.py:247
  178.5 21.9 %collective-permute-start.28 = (bf16[384,256]{1,0:T(8,128)(2,1)S(1)}, bf16[384,256]{1,0:T(8,128)(2,1)S(1)}, u32[]{:S(2)}, u32[]{:S(2)}) collective-permute-start(bf16[384,256]{1,0:T(8,128)(2,1)S(1)} %add_convert_fusion.4), channel_id=1, source_target_pairs={{0,8},{8,16},{16,24},{24,0},{1,9},{9,17},{17,25},{25,1},{2,10},{10... | collective-permute-start | bytes 589832 | tf_op jit(solution)/shard_map/ppermute | solution.py:247
  191.4 9.0 %collective-permute-start.29 = (bf16[384,256]{1,0:T(8,128)(2,1)S(1)}, bf16[384,256]{1,0:T(8,128)(2,1)S(1)}, u32[]{:S(2)}, u32[]{:S(2)}) collective-permute-start(bf16[384,256]{1,0:T(8,128)(2,1)S(1)} %add_convert_fusion.4), channel_id=1, source_target_pairs={{0,16},{8,24},{16,0},{24,8},{1,17},{9,25},{17,1},{25,9},{2,18},{10... | collective-permute-start | bytes 589832 | tf_op jit(solution)/shard_map/ppermute | solution.py:247
  192.8 7.6 %collective-permute-start.30 = (bf16[384,256]{1,0:T(8,128)(2,1)S(1)}, bf16[384,256]{1,0:T(8,128)(2,1)S(1)}, u32[]{:S(2)}, u32[]{:S(2)}) collective-permute-start(bf16[384,256]{1,0:T(8,128)(2,1)S(1)} %add_convert_fusion.4), channel_id=1, source_target_pairs={{0,24},{8,0},{16,8},{24,16},{1,25},{9,1},{17,9},{25,17},{2,26},{10... | collective-permute-start | bytes 589832 | tf_op jit(solution)/shard_map/ppermute | solution.py:247
  192.8 5.4 %collective-permute-start.19 = (bf16[256,256]{1,0:T(8,128)(2,1)S(1)}, bf16[256,256]{1,0:T(8,128)(2,1)S(1)}, u32[]{:S(2)}, u32[]{:S(2)}) collective-permute-start(bf16[256,256]{1,0:T(8,128)(2,1)S(1)} %get-tuple-element.79), channel_id=1, source_target_pairs={{0,32},{32,64},{64,96},{96,128},{128,160},{160,192},{192,224},{224... | collective-permute-start | bytes 393224 | tf_op jit(solution)/shard_map/ppermute | solution.py:247
  195.0 4.3 %collective-permute-start.20 = (bf16[256,256]{1,0:T(8,128)(2,1)S(1)}, bf16[256,256]{1,0:T(8,128)(2,1)S(1)}, u32[]{:S(2)}, u32[]{:S(2)}) collective-permute-start(bf16[256,256]{1,0:T(8,128)(2,1)S(1)} %get-tuple-element.78), channel_id=1, source_target_pairs={{0,224},{32,0},{64,32},{96,64},{128,96},{160,128},{192,160},{224,1... | collective-permute-start | bytes 393224 | tf_op jit(solution)/shard_map/ppermute | solution.py:247
  200.8 3.7 %collective-permute-start.31 = (bf16[6,256,256]{2,1,0:T(8,128)(2,1)S(1)}, bf16[6,256,256]{2,1,0:T(8,128)(2,1)S(1)}, u32[]{:S(2)}, u32[]{:S(2)}) collective-permute-start(bf16[6,256,256]{2,1,0:T(8,128)(2,1)S(1)} %bitcast.109), channel_id=1, source_target_pairs={{0,4},{4,0},{1,5},{5,1},{2,6},{6,2},{3,7},{7,3},{8,12},{12,8},{9,1... | collective-permute-start | bytes 2359304 | tf_op jit(solution)/shard_map/ppermute | solution.py:247
  (17 other events, 203.9 us)
where the time goes:
time: 207 us
  waiting for transfers between devices  63.6 us (31%)
  starting transfers between devices  42.6 us (21%)
  blocking collectives  36 us (17%)
  Pallas kernels  31.8 us (15%)
  other arithmetic  16.4 us (8%)
  matrix products  6.77 us (3%)
  local copies, waits for them, and re-layouts  6.42 us (3%)
  between operations  2.91 us (1%)
    ppermute x29, waiting for transfers between devices, shift(): lax.ppermute(values, axis, [(i, (i + by) % size) for i in range(size)])  48.2 us
    ppermute x29, starting transfers between devices, shift(): lax.ppermute(values, axis, [(i, (i + by) % size) for i in range(size)])  39.2 us
    all_to_all x1, blocking collectives, exchange(): return lax.all_to_all(values, axis, 0, 0, tiled=True)  36 us
    pallas_call x1, Pallas kernels, score(): pl.pallas_call(lambda *refs: score_kernel(*refs, positions=positions, per...  18.8 us
    ppermute x3, waiting for transfers between devices, pair(): return lax.ppermute(values, axis, [(i, i ^ bit) for i in range(size)])  15.3 us
    pallas_call x1, Pallas kernels, make_queries(): pl.pallas_call(lambda *refs: query_kernel(*refs, groups=groups), out_shap...  7.75 us
    pallas_call x1, Pallas kernels, head_product(): pl.pallas_call(head_kernel, out_shape=(half, half, jax.ShapeDtypeStruct((...  5.25 us
  transfers between devices with their start and end apart: 32, of which 16 were waited for; matrix products, arithmetic and copies ran while one was open for 9% of the time, Pallas kernels for 6%

commit v1 on v0

--- a/solution.py
+++ b/solution.py
@@ -52,9 +52,7 @@
     return (target, context)
 
 
-def query_kernel(
-    tgt_ref, ctx_ref, hw_ref, q_ref, t_ref, inv_ref, exp_ref, ten_ref, pad_s, *, groups
-):
+def query_kernel(tgt_ref, ctx_ref, hw_ref, q_ref, t_ref, stat_ref, pad_s, *, groups):
     positions, channels = tgt_ref.shape
     horizon = hw_ref.shape[0]
     rows = positions // groups
@@ -74,9 +72,9 @@
         part = pl.ds(pl.multiple_of(k * rows, rows), rows)
         q_ref[:, part, :] = query.reshape(groups, rows, -1)
         t_ref[:, part, :] = shifted.astype(BF).reshape(groups, rows, -1)
-        inv_ref[:, part, :] = inv.reshape(groups, rows, 1)
-        exp_ref[:, part, :] = jnp.exp(score).reshape(groups, rows, 1)
-        ten_ref[:, part, :] = usable.reshape(groups, rows, 1)
+        stat_ref[:, part, 0:1] = inv.reshape(groups, rows, 1)
+        stat_ref[:, part, 1:2] = jnp.exp(score).reshape(groups, rows, 1)
+        stat_ref[:, part, 2:3] = usable.reshape(groups, rows, 1)
 
     def steps(i, carry):
         for j in range(unroll):
@@ -87,16 +85,15 @@
     lax.fori_loop(0, horizon // unroll, steps, 0)
 
 
-def score_kernel(
-    where_ref, q_ref, t_ref, inv_ref, exp_ref, ten_ref, *rest, positions, per_group, bank_count
-):
+def score_kernel(where_ref, q_ref, t_ref, stat_ref, *rest, per_group, bank_count):
     banks = rest[:bank_count]
     keep_ref, send_ref, pg_ref, p_ref = rest[bank_count : bank_count + 4]
     nbuf, blocks_s, sems, out_sems = rest[bank_count + 4 :]
-    groups = q_ref.shape[0]
+    batch = q_ref.shape[0]
     horizon = pg_ref.shape[0]
-    rows = positions // groups
-    entries = groups * per_group
+    rows = pg_ref.shape[1] // batch
+    entries = nbuf.shape[0]
+    at = pl.program_id(0)
 
     def start(e, carry):
         bank_id = where_ref[0, e]
@@ -109,52 +106,62 @@
 
         return carry
 
-    lax.fori_loop(0, entries, start, 0)
-    blocks_s[...] = jnp.zeros(blocks_s.shape, BF)
-
-    def group(g, carry):
-        for s in range(per_group):
-            e = g * per_group + s
-            pltpu.make_async_copy(banks[0].at[0], nbuf.at[e], sems.at[e]).wait()
-        queries = q_ref[g]
-        negatives = nbuf[pl.ds(g * per_group, per_group)].reshape(per_group * 128, -1)
+    def arrive(e, carry):
+        pltpu.make_async_copy(banks[0].at[0], nbuf.at[e], sems.at[e]).wait()
+        return carry
+
+    @pl.when(at == 0)
+    def _():
+        lax.fori_loop(0, entries, start, 0)
+        blocks_s[...] = jnp.zeros(blocks_s.shape, BF)
+        lax.fori_loop(0, entries, arrive, 0)
+
+    def weights(j):
+        first = (at * batch + j) * per_group
+        queries = q_ref[j]
+        stat = stat_ref[j]
+        pos_exp, ten = stat[:, 1:2], stat[:, 2:3]
+        negatives = nbuf[pl.ds(first, per_group)].reshape(per_group * 128, -1)
         negative = lax.dot_general(
             queries, negatives, (((1,), (1,)), ((), ())), preferred_element_type=F32
         )
         neg_exp = jnp.exp2((10.0 * math.log2(math.e)) * negative)
-        pos_exp = exp_ref[g]
-        over = ten_ref[g] / (pos_exp + jnp.sum(neg_exp, -1, keepdims=True))
+        over = ten / (pos_exp + jnp.sum(neg_exp, -1, keepdims=True))
         weight = (neg_exp * over).astype(BF)
-        pos_weight = pos_exp * over - ten_ref[g]
+        pos_weight = pos_exp * over - ten
         neg_part = jnp.dot(weight, negatives, preferred_element_type=F32)
         neg_grad = lax.dot_general(
             weight, queries, (((0,), (0,)), ((), ())), preferred_element_type=F32
         )
+        return queries, pos_weight, neg_part, neg_grad
+
+    def finish(j, queries, pos_weight, neg_part, neg_grad):
+        unit = queries.astype(F32)
+        query_grad = pos_weight * t_ref[j].astype(F32) + neg_part
+        radial = jnp.sum(unit * query_grad, -1, keepdims=True)
+        pred_grad = ((query_grad - unit * radial) * stat_ref[j][:, 0:1]).astype(BF)
+        pos_term = (pos_weight * unit).astype(BF)
+        for k in range(horizon):
+            pg_ref[k, j * rows : (j + 1) * rows, :] = pred_grad[k * rows : (k + 1) * rows]
+            p_ref[k, j * rows : (j + 1) * rows, :] = pos_term[k * rows : (k + 1) * rows]
         for s in range(per_group):
-            e = g * per_group + s
-            place = where_ref[2, e]
+            place = where_ref[2, (at * batch + j) * per_group + s]
             block = neg_grad[s * 128 : (s + 1) * 128]
             blocks_s[place] = (blocks_s[place].astype(F32) + block).astype(BF)
 
-        unit = queries.astype(F32)
-        query_grad = pos_weight * t_ref[g].astype(F32) + neg_part
-        radial = jnp.sum(unit * query_grad, -1, keepdims=True)
-        pred_grad = ((query_grad - unit * radial) * inv_ref[g]).astype(BF)
-        pos_term = pos_weight * unit
-        at = pl.ds(pl.multiple_of(g * rows, rows), rows)
-        for k in range(horizon):
-            pg_ref[k, at, :] = pred_grad[k * rows : (k + 1) * rows]
-            p_ref[k, at, :] = pos_term[k * rows : (k + 1) * rows]
-        return carry
-
-    lax.fori_loop(0, groups, group, 0)
-    half = blocks_s.shape[0] // 2
-    sent = pltpu.make_async_copy(blocks_s.at[pl.ds(half, half)], send_ref, out_sems.at[0])
-    kept = pltpu.make_async_copy(blocks_s.at[pl.ds(0, half)], keep_ref, out_sems.at[1])
-    sent.start()
-    kept.start()
-    sent.wait()
-    kept.wait()
+    made = [weights(j) for j in range(batch)]
+    for j in range(batch):
+        finish(j, *made[j])
+
+    @pl.when(at == pl.num_programs(0) - 1)
+    def _():
+        half = blocks_s.shape[0] // 2
+        sent = pltpu.make_async_copy(blocks_s.at[pl.ds(half, half)], send_ref, out_sems.at[0])
+        kept = pltpu.make_async_copy(blocks_s.at[pl.ds(0, half)], keep_ref, out_sems.at[1])
+        sent.start()
+        kept.start()
+        sent.wait()
+        kept.wait()
 
 
 def head_kernel(core_ref, ctx_ref, pg_ref, p_ref, hkeep_ref, hsend_ref, pos_ref, pad_s):
@@ -177,7 +184,7 @@
     pad_s[...] = jnp.zeros(pad_s.shape, F32)
     for k in range(p_ref.shape[0]):
         at = slice(k + 1, k + 1 + positions)
-        pad_s[at] = pad_s[at] + p_ref[k]
+        pad_s[at] = pad_s[at] + p_ref[k].astype(F32)
     pos_ref[...] = pad_s[:positions]
 
 
@@ -190,34 +197,43 @@
         out_shape=(
             jax.ShapeDtypeStruct((groups, rows, channels), BF),
             jax.ShapeDtypeStruct((groups, rows, channels), BF),
-            jax.ShapeDtypeStruct((groups, rows, 1), F32),
-            jax.ShapeDtypeStruct((groups, rows, 1), F32),
-            jax.ShapeDtypeStruct((groups, rows, 1), F32),
+            jax.ShapeDtypeStruct((groups, rows, 3), F32),
         ),
         in_specs=[vmem] * 3,
-        out_specs=(vmem,) * 5,
+        out_specs=(vmem,) * 3,
         scratch_shapes=[pltpu.VMEM((positions + 16, channels), F32)],
         name="queries",
     )(target, context, head_maps)
 
 
 def score(where, made, banks, horizon, positions, per_group):
-    groups, _, channels = made[0].shape
+    groups, queries, channels = made[0].shape
     blocks = 2 * (positions // 128) * banks[0].shape[0]
-    vmem = pl.BlockSpec(memory_space=pltpu.VMEM)
+    batch = math.gcd(groups, 2)
+    span = batch * (positions // groups)
     hbm = pl.BlockSpec(memory_space=pl.ANY)
+
+    def by_group(width):
+        return pl.BlockSpec((batch, queries, width), lambda i: (i, 0, 0))
+
+    by_position = pl.BlockSpec((horizon, span, channels), lambda i: (0, i, 0))
     return pl.pallas_call(
-        lambda *refs: score_kernel(
-            *refs, positions=positions, per_group=per_group, bank_count=len(banks)
-        ),
+        lambda *refs: score_kernel(*refs, per_group=per_group, bank_count=len(banks)),
+        grid=(groups // batch,),
         out_shape=(
             jax.ShapeDtypeStruct((blocks, 128, channels), BF),
             jax.ShapeDtypeStruct((blocks, 128, channels), BF),
             jax.ShapeDtypeStruct((horizon, positions, channels), BF),
-            jax.ShapeDtypeStruct((horizon, positions, channels), F32),
+            jax.ShapeDtypeStruct((horizon, positions, channels), BF),
         ),
-        in_specs=[pl.BlockSpec(memory_space=pltpu.SMEM)] + [vmem] * 5 + [hbm] * len(banks),
-        out_specs=(hbm, hbm, vmem, vmem),
+        in_specs=[
+            pl.BlockSpec(memory_space=pltpu.SMEM),
+            by_group(channels),
+            by_group(channels),
+            by_group(made[2].shape[-1]),
+        ]
+        + [hbm] * len(banks),
+        out_specs=(hbm, hbm, by_position, by_position),
         scratch_shapes=[
             pltpu.VMEM((groups * per_group, 128, channels), BF),
             pltpu.VMEM((2 * blocks, 128, channels), BF),
@@ -306,10 +322,11 @@
     for i, (first, count) in enumerate(zip(starts, Z_BUNDLES)):
         span = slice(first, first + count)
         low, high, keep, received = lax.optimization_barrier((*firsts[i], keep, received))
-        ahead = add(keep[1, span], received[1, span])
-        behind = add(keep[3, span], received[3, span])
-        ahead = jnp.concatenate([add(ahead[:, :128], low), ahead[:, 128:]], 1).astype(BF)
-        behind = jnp.concatenate([behind[:, :128], add(behind[:, 128:], high)], 1).astype(BF)
+        rest = keep.shape[2] - 128
+        low = jnp.pad(low, ((0, 0), (0, rest), (0, 0)))
+        high = jnp.pad(high, ((0, 0), (rest, 0), (0, 0)))
+        ahead = add(keep[1, span], received[1, span], low).astype(BF)
+        behind = add(keep[3, span], received[3, span], high).astype(BF)
         seconds.append([shift(ahead, "x", 1), shift(behind, "x", -1)])
     for i, (first, count) in enumerate(zip(starts, Z_BUNDLES)):
         span = slice(first, first + count)

time: 207 us -> 204 us (0.986)
  Pallas kernels: 31.8 us -> 27.5 us
    convert_element_type x0 -> x1, other arithmetic: none -> 3.92 us  [exchange_back(): ahead = add(keep[1, span], received[1, span], low).astype(BF)]
    add x1 -> x0, other arithmetic: 2.91 us -> none  [add(): total = total + term.astype(F32)]
    pallas_call x1, Pallas kernels: 18.8 us -> 16 us  [score(): pl.pallas_call(lambda *refs: score_kernel(*refs, per_group=per_group, ban...]
    ppermute x29, starting transfers between devices: 39.2 us -> 41.6 us  [shift(): lax.ppermute(values, axis, [(i, (i + by) % size) for i in range(size)])]
    ppermute x3, waiting for transfers between devices: 15.3 us -> 13.1 us  [pair(): return lax.ppermute(values, axis, [(i, i ^ bit) for i in range(size)])]
    ppermute x29, waiting for transfers between devices: 48.2 us -> 50.3 us  [shift(): lax.ppermute(values, axis, [(i, (i + by) % size) for i in range(size)])]
  transfers between devices with their start and end apart: 32 -> 32, of which waited for: 16 -> 15; matrix products, arithmetic and copies ran while one was open for 9% -> 9% of each run, Pallas kernels for 6% -> 6%
where the time goes in v1:
time: 204 us; the launch traced here: 203 us
  waiting for transfers between devices  63.4 us (31%)
  starting transfers between devices  44.5 us (22%)
  blocking collectives  36.1 us (18%)
  Pallas kernels  27.5 us (13%)
  other arithmetic  16 us (8%)
  matrix products  6.77 us (3%)
  local copies, waits for them, and re-layouts  6.17 us (3%)
  between operations  2.84 us (1%)
    ppermute x29, waiting for transfers between devices, shift(): lax.ppermute(values, axis, [(i, (i + by) % size) for i in range(size)])  50.3 us
    ppermute x29, starting transfers between devices, shift(): lax.ppermute(values, axis, [(i, (i + by) % size) for i in range(size)])  41.6 us
    all_to_all x1, blocking collectives, exchange(): return lax.all_to_all(values, axis, 0, 0, tiled=True)  36.1 us
    pallas_call x1, Pallas kernels, score(): pl.pallas_call(lambda *refs: score_kernel(*refs, per_group=per_group, ban...  16 us
    ppermute x3, waiting for transfers between devices, pair(): return lax.ppermute(values, axis, [(i, i ^ bit) for i in range(size)])  13.1 us
    pallas_call x1, Pallas kernels, make_queries(): pl.pallas_call(lambda *refs: query_kernel(*refs, groups=groups), out_shap...  6.73 us
    pallas_call x1, Pallas kernels, head_product(): pl.pallas_call(head_kernel, out_shape=(half, half, jax.ShapeDtypeStruct((...  4.76 us
  transfers between devices with their start and end apart: 32, of which 15 were waited for; matrix products, arithmetic and copies ran while one was open for 9% of the time, Pallas kernels for 6%

profile of v1, /device:TPU:1, one launch (start us, length us, event | category | flops | bytes accessed | tf_op | source)
XLA Modules:
  0.0 203.3 jit_solution(8983003863155409823)
XLA Ops:
  1.9 3.1 %fusion.5 = bf16[1024,256]{1,0:T(8,128)(2,1)S(1)} fusion(bf16[1024,5]{1,0:T(8,128)(2,1)S(1)} %reshape_reshape.3, bf16[5,256]{1,0:T(8,128)(2,1)} %param.9), kind=kOutput, calls=%fused_computation.12 | convolution fusion | flops 19660800 | bytes 537088 | tf_op jit(solution)/shard_map/dot_general | solution.py:24
  7.7 36.1 %all_to_all.5 = bf16[8,256,256]{2,1,0:T(8,128)(2,1)S(1)} all-to-all(bf16[8,256,256]{2,1,0:T(8,128)(2,1)S(1)} %broadcast_in_dim.12), channel_id=1, replica_groups=mesh['z'=8,'x'=4,'c'=2,'rep'=4] {'z'}, dimensions={0} | all-to-all | bytes 2097152 | tf_op jit(solution)/shard_map/all_to_all | solution.py:267
  48.6 6.7 %queries.1 = (bf16[8,384,256]{2,1,0:T(8,128)(2,1)}, bf16[8,384,256]{2,1,0:T(8,128)(2,1)}, f32[8,384,3]{2,1,0:T(8,128)}) custom-call(bf16[256,256]{1,0:T(8,128)(2,1)} %copy-done.4, bf16[256,256]{1,0:T(8,128)(2,1)} %fusion.38.refs_1_.ctx_ref, bf16[12,256,256]{2,1,0:T(8,128)(2,1)} %bitcast.117), custom_call_target="tpu_custom_call" | custom-call | tf_op jit(solution)/shard_map/queries/pallas_call | solution.py:195
  55.3 11.8 %collective-permute-done = bf16[8,256,256]{2,1,0:T(8,128)(2,1)S(1)} collective-permute-done((bf16[8,256,256]{2,1,0:T(8,128)(2,1)S(1)}, bf16[8,256,256]{2,1,0:T(8,128)(2,1)S(1)}, u32[]{:S(2)}, u32[]{:S(2)}) %collective-permute-start) | collective-permute-done | bytes 1048608 | tf_op jit(solution)/shard_map/ppermute | solution.py:263
  69.8 1.7 collective-permute-start.3
  71.6 3.9 %collective-permute-start.4 = (bf16[8,256,256]{2,1,0:T(8,128)(2,1)S(1)}, bf16[8,256,256]{2,1,0:T(8,128)(2,1)}, u32[]{:S(2)}, u32[]{:S(2)}) collective-permute-start(bf16[8,256,256]{2,1,0:T(8,128)(2,1)S(1)} %all_to_all.5), channel_id=1, source_target_pairs={{0,4},{4,0},{1,5},{5,1},{2,6},{6,2},{3,7},{7,3},{8,12},{12,8},{9,1... | collective-permute-start | bytes 3145736 | tf_op jit(solution)/shard_map/ppermute | solution.py:263
  76.4 3.2 %collective-permute-done.2.refs_7_ = bf16[8,128,256]{2,1,0:T(8,128)(2,1)} collective-permute-done((bf16[8,128,256]{2,1,0:T(8,128)(2,1)}, bf16[8,128,256]{2,1,0:T(8,128)(2,1)}, u32[]{:S(2)}, u32[]{:S(2)}) %collective-permute-start.2) | collective-permute-done | bytes 524320 | tf_op jit(solution)/shard_map/ppermute | solution.py:263
  79.6 4.3 %collective-permute-start.7 = (bf16[8,128,256]{2,1,0:T(8,128)(2,1)}, bf16[8,128,256]{2,1,0:T(8,128)(2,1)S(1)}, u32[]{:S(2)}, u32[]{:S(2)}) collective-permute-start(bf16[8,128,256]{2,1,0:T(8,128)(2,1)} %collective-permute-done.2.refs_7_), channel_id=1, source_target_pairs={{0,4},{4,0},{1,5},{5,1},{2,6},{6,2},{3,7},{7,3},{8,12},{12,8},{9,1... | collective-permute-start | bytes 1572872 | tf_op jit(solution)/shard_map/ppermute | solution.py:263
  87.2 16.0 %score.1 = (bf16[64,128,256]{2,1,0:T(8,128)(2,1)}, bf16[64,128,256]{2,1,0:T(8,128)(2,1)}, bf16[12,256,256]{2,1,0:T(8,128)(2,1)}, bf16[12,256,256]{2,1,0:T(8,128)(2,1)}) custom-call(s32[3,32]{1,0:T(4,128)} %pad_add_fusion.refs_0_, bf16[8,384,256]{2,1,0:T(8,128)(2,1)} %get-tuple-element.32.refs_1_, bf16[8,384,256]{2,1,0:T(8,128)(2,1)} %get-tuple-element.33.refs_2_, ...), custom_call_target="tpu_custom_call" | custom-call | tf_op jit(solution)/shard_map/score/pallas_call | solution.py:220
  103.7 4.8 %heads.1 = (bf16[6,256,256]{2,1,0:T(8,128)(2,1)}, bf16[6,256,256]{2,1,0:T(8,128)(2,1)}, f32[256,256]{1,0:T(8,128)}) custom-call(s32[1]{0:T(128)} %bitcast.core_ref, bf16[256,256]{1,0:T(8,128)(2,1)} %fusion.38.refs_1_.ctx_ref, bf16[12,256,256]{2,1,0:T(8,128)(2,1)} %get-tuple-element.37.pg_ref, bf16[12,256,256]{2,1,0:T(8,128)(2,1)} %get-tuple-element.38.p_ref), custom_call_target="tpu_custom_call" | custom-call | tf_op jit(solution)/shard_map/heads/pallas_call | solution.py:251
  108.6 2.2 %collective-permute-done.9 = bf16[4,8,256,256]{3,2,1,0:T(8,128)(2,1)} collective-permute-done((bf16[4,8,256,256]{3,2,1,0:T(8,128)(2,1)}, bf16[4,8,256,256]{3,2,1,0:T(8,128)(2,1)}, u32[]{:S(2)}, u32[]{:S(2)}) %collective-permute-start.9) | collective-permute-done | bytes 4194336 | tf_op jit(solution)/shard_map/ppermute | solution.py:263
  110.9 2.7 %fusion.17 = (bf16[8,128,256]{2,1,0:T(8,128)(2,1)}, bf16[8,128,256]{2,1,0:T(8,128)(2,1)S(1)}) fusion(bf16[4,8,256,256]{3,2,1,0:T(8,128)(2,1)} %collective-permute-done.9, bf16[4,8,256,256]{3,2,1,0:T(8,128)(2,1)} %bitcast.106), kind=kLoop, calls=%fused_computation.38 | loop fusion | flops 2097152 | bytes 3145728 | tf_op jit(solution)/shard_map/convert_element_type | solution.py:320
  113.5 2.8 %collective-permute-start.11 = (bf16[8,128,256]{2,1,0:T(8,128)(2,1)}, bf16[8,128,256]{2,1,0:T(8,128)(2,1)S(1)}, u32[]{:S(2)}, u32[]{:S(2)}) collective-permute-start(bf16[8,128,256]{2,1,0:T(8,128)(2,1)} %get-tuple-element.66), channel_id=1, source_target_pairs={{0,24},{8,0},{16,8},{24,16},{1,25},{9,1},{17,9},{25,17},{2,26},{10... | collective-permute-start | bytes 1572872 | tf_op jit(solution)/shard_map/ppermute | solution.py:263
  116.6 2.7 %collective-permute-start.23 = (bf16[384,256]{1,0:T(8,128)(2,1)S(1)}, bf16[384,256]{1,0:T(8,128)(2,1)S(1)}, u32[]{:S(2)}, u32[]{:S(2)}) collective-permute-start(bf16[384,256]{1,0:T(8,128)(2,1)S(1)} %get-tuple-element.83), channel_id=1, source_target_pairs={{0,24},{8,0},{16,8},{24,16},{1,25},{9,1},{17,9},{25,17},{2,26},{10... | collective-permute-start | bytes 589832 | tf_op jit(solution)/shard_map/ppermute | solution.py:263
  120.5 7.1 %collective-permute-done.11 = bf16[8,128,256]{2,1,0:T(8,128)(2,1)S(1)} collective-permute-done((bf16[8,128,256]{2,1,0:T(8,128)(2,1)}, bf16[8,128,256]{2,1,0:T(8,128)(2,1)S(1)}, u32[]{:S(2)}, u32[]{:S(2)}) %collective-permute-start.11) | collective-permute-done | bytes 524320 | tf_op jit(solution)/shard_map/ppermute | solution.py:263
  127.5 2.8 %collective-permute-done.10 = bf16[8,128,256]{2,1,0:T(8,128)(2,1)S(1)} collective-permute-done((bf16[8,128,256]{2,1,0:T(8,128)(2,1)S(1)}, bf16[8,128,256]{2,1,0:T(8,128)(2,1)S(1)}, u32[]{:S(2)}, u32[]{:S(2)}) %collective-permute-start.10) | collective-permute-done | bytes 524320 | tf_op jit(solution)/shard_map/ppermute | solution.py:263
  130.3 3.9 %fusion.1 = (bf16[8,256,256]{2,1,0:T(8,128)(2,1)S(1)}, bf16[8,256,256]{2,1,0:T(8,128)(2,1)}) fusion(bf16[8,128,256]{2,1,0:T(8,128)(2,1)S(1)} %collective-permute-done.10, bf16[4,8,256,256]{3,2,1,0:T(8,128)(2,1)} %collective-permute-done.9, bf16[4,8,256,256]{3,2,1,0:T(8,128)(2,1)} %bitcast.107, bf16[8,128,256]{2,1,0:T(8,128)(2,1)S(1)} %collective-permute-done.11), kind=kLoop, calls=%fused_computation.4 | loop fusion | flops 6291456 | bytes 7340032 | tf_op jit(solution)/shard_map/convert_element_type | solution.py:328
  135.7 2.4 %collective-permute-done.22 = bf16[384,256]{1,0:T(8,128)(2,1)S(1)} collective-permute-done((bf16[384,256]{1,0:T(8,128)(2,1)S(1)}, bf16[384,256]{1,0:T(8,128)(2,1)S(1)}, u32[]{:S(2)}, u32[]{:S(2)}) %collective-permute-start.22) | collective-permute-done | bytes 196640 | tf_op jit(solution)/shard_map/ppermute | solution.py:263
  140.1 3.1 %collective-permute-done.25 = bf16[384,256]{1,0:T(8,128)(2,1)S(1)} collective-permute-done((bf16[384,256]{1,0:T(8,128)(2,1)S(1)}, bf16[384,256]{1,0:T(8,128)(2,1)S(1)}, u32[]{:S(2)}, u32[]{:S(2)}) %collective-permute-start.25) | collective-permute-done | bytes 196640 | tf_op jit(solution)/shard_map/ppermute | solution.py:291
  144.0 10.0 %collective-permute-done.26 = bf16[384,256]{1,0:T(8,128)(2,1)} collective-permute-done((bf16[384,256]{1,0:T(8,128)(2,1)}, bf16[384,256]{1,0:T(8,128)(2,1)}, u32[]{:S(2)}, u32[]{:S(2)}) %collective-permute-start.26) | collective-permute-done | bytes 196640 | tf_op jit(solution)/shard_map/ppermute | solution.py:291
  155.1 2.6 %collective-permute-start.27 = (bf16[384,256]{1,0:T(8,128)(2,1)S(1)}, bf16[384,256]{1,0:T(8,128)(2,1)S(1)}, u32[]{:S(2)}, u32[]{:S(2)}) collective-permute-start(bf16[384,256]{1,0:T(8,128)(2,1)S(1)} %add_convert_fusion.6), channel_id=1, source_target_pairs={{0,128},{32,160},{64,192},{96,224},{128,0},{160,32},{192,64},{224,... | collective-permute-start | bytes 589832 | tf_op jit(solution)/shard_map/ppermute | solution.py:291
  158.9 1.6 collective-permute-done.12
  160.5 2.1 %fusion.92 = (bf16[8,256,256]{2,1,0:T(8,128)(2,1)S(1)}, f32[8,256,256]{2,1,0:T(8,128)S(1)}) fusion(bf16[8,256,256]{2,1,0:T(8,128)(2,1)S(1)} %collective-permute-done.13, bf16[8,256,256]{2,1,0:T(8,128)(2,1)S(1)} %collective-permute-done.12, bf16[4,8,256,256]{3,2,1,0:T(8,128)(2,1)} %collective-permute-done.9, bf16[4,8,256,256]{3,2,1,0:T(8,128)(2,1)} %bitcast.108), kind=kLoop, calls=%fused_computation.188 | loop fusion | flops 4194304 | bytes 7340032 | tf_op jit(solution)/shard_map/convert.7
  162.6 2.5 %collective-permute-start.14 = (bf16[256,256]{1,0:T(8,128)(2,1)S(1)}, bf16[256,256]{1,0:T(8,128)(2,1)S(1)}, u32[]{:S(2)}, u32[]{:S(2)}) collective-permute-start(bf16[256,256]{1,0:T(8,128)(2,1)S(1)} %get-tuple-element.76), channel_id=1, source_target_pairs={{0,128},{32,160},{64,192},{96,224},{128,0},{160,32},{192,64},{224,... | collective-permute-start | bytes 393224 | tf_op jit(solution)/shard_map/ppermute | solution.py:263
  165.3 4.3 %collective-permute-start.16 = (bf16[256,256]{1,0:T(8,128)(2,1)S(1)}, bf16[256,256]{1,0:T(8,128)(2,1)S(1)}, u32[]{:S(2)}, u32[]{:S(2)}) collective-permute-start(bf16[256,256]{1,0:T(8,128)(2,1)S(1)} %get-tuple-element.74), channel_id=1, source_target_pairs={{0,160},{32,192},{64,224},{96,0},{128,32},{160,64},{192,96},{224,1... | collective-permute-start | bytes 393224 | tf_op jit(solution)/shard_map/ppermute | solution.py:263
  169.6 2.4 %collective-permute-start.17 = (bf16[256,256]{1,0:T(8,128)(2,1)S(1)}, bf16[256,256]{1,0:T(8,128)(2,1)S(1)}, u32[]{:S(2)}, u32[]{:S(2)}) collective-permute-start(bf16[256,256]{1,0:T(8,128)(2,1)S(1)} %get-tuple-element.73), channel_id=1, source_target_pairs={{0,64},{32,96},{64,128},{96,160},{128,192},{160,224},{192,0},{224,... | collective-permute-start | bytes 393224 | tf_op jit(solution)/shard_map/ppermute | solution.py:263
  173.6 13.0 %collective-permute-done.15 = bf16[256,256]{1,0:T(8,128)(2,1)S(1)} collective-permute-done((bf16[256,256]{1,0:T(8,128)(2,1)S(1)}, bf16[256,256]{1,0:T(8,128)(2,1)S(1)}, u32[]{:S(2)}, u32[]{:S(2)}) %collective-permute-start.15) | collective-permute-done | bytes 131104 | tf_op jit(solution)/shard_map/ppermute | solution.py:263
  186.6 2.9 %collective-permute-start.29 = (bf16[384,256]{1,0:T(8,128)(2,1)S(1)}, bf16[384,256]{1,0:T(8,128)(2,1)S(1)}, u32[]{:S(2)}, u32[]{:S(2)}) collective-permute-start(bf16[384,256]{1,0:T(8,128)(2,1)S(1)} %add_convert_fusion.4), channel_id=1, source_target_pairs={{0,16},{8,24},{16,0},{24,8},{1,17},{9,25},{17,1},{25,9},{2,18},{10... | collective-permute-start | bytes 589832 | tf_op jit(solution)/shard_map/ppermute | solution.py:263
  189.6 2.7 %collective-permute-start.20 = (bf16[256,256]{1,0:T(8,128)(2,1)S(1)}, bf16[256,256]{1,0:T(8,128)(2,1)S(1)}, u32[]{:S(2)}, u32[]{:S(2)}) collective-permute-start(bf16[256,256]{1,0:T(8,128)(2,1)S(1)} %get-tuple-element.70), channel_id=1, source_target_pairs={{0,224},{32,0},{64,32},{96,64},{128,96},{160,128},{192,160},{224,1... | collective-permute-start | bytes 393224 | tf_op jit(solution)/shard_map/ppermute | solution.py:263
  192.3 2.6 %collective-permute-done.19 = bf16[256,256]{1,0:T(8,128)(2,1)S(1)} collective-permute-done((bf16[256,256]{1,0:T(8,128)(2,1)S(1)}, bf16[256,256]{1,0:T(8,128)(2,1)S(1)}, u32[]{:S(2)}, u32[]{:S(2)}) %collective-permute-start.19) | collective-permute-done | bytes 131104 | tf_op jit(solution)/shard_map/ppermute | solution.py:263
  197.7 1.6 collective-permute-start.31
  201.3 2.0 convert_multiply_fusion
  (112 shorter events, 29.0 us)
Async XLA Ops:
  43.7 23.4 %collective-permute-start = (bf16[8,256,256]{2,1,0:T(8,128)(2,1)S(1)}, bf16[8,256,256]{2,1,0:T(8,128)(2,1)S(1)}, u32[]{:S(2)}, u32[]{:S(2)}) collective-permute-start(bf16[8,256,256]{2,1,0:T(8,128)(2,1)S(1)} %all_to_all.5), channel_id=1, source_target_pairs={{0,8},{8,16},{16,24},{24,0},{1,9},{9,17},{17,25},{25,1},{2,10},{10... | collective-permute-start | bytes 3145736 | tf_op jit(solution)/shard_map/ppermute | solution.py:263
  44.9 22.2 %collective-permute-start.1 = (bf16[8,256,256]{2,1,0:T(8,128)(2,1)S(1)}, bf16[8,256,256]{2,1,0:T(8,128)(2,1)S(1)}, u32[]{:S(2)}, u32[]{:S(2)}) collective-permute-start(bf16[8,256,256]{2,1,0:T(8,128)(2,1)S(1)} %all_to_all.5), channel_id=1, source_target_pairs={{0,24},{8,0},{16,8},{24,16},{1,25},{9,1},{17,9},{25,17},{2,26},{10... | collective-permute-start | bytes 3145736 | tf_op jit(solution)/shard_map/ppermute | solution.py:263
  68.0 11.6 %collective-permute-start.2 = (bf16[8,128,256]{2,1,0:T(8,128)(2,1)}, bf16[8,128,256]{2,1,0:T(8,128)(2,1)}, u32[]{:S(2)}, u32[]{:S(2)}) collective-permute-start(bf16[8,128,256]{2,1,0:T(8,128)(2,1)} %slice.100), channel_id=1, source_target_pairs={{0,8},{8,16},{16,24},{24,0},{1,9},{9,17},{17,25},{25,1},{2,10},{10... | collective-permute-start | bytes 1572872 | tf_op jit(solution)/shard_map/ppermute | solution.py:263
  69.8 14.1 %collective-permute-start.3 = (bf16[8,128,256]{2,1,0:T(8,128)(2,1)}, bf16[8,128,256]{2,1,0:T(8,128)(2,1)}, u32[]{:S(2)}, u32[]{:S(2)}) collective-permute-start(bf16[8,128,256]{2,1,0:T(8,128)(2,1)} %slice.101), channel_id=1, source_target_pairs={{0,24},{8,0},{16,8},{24,16},{1,25},{9,1},{17,9},{25,17},{2,26},{10... | collective-permute-start | bytes 1572872 | tf_op jit(solution)/shard_map/ppermute | solution.py:263
  71.6 13.5 %collective-permute-start.4 = (bf16[8,256,256]{2,1,0:T(8,128)(2,1)S(1)}, bf16[8,256,256]{2,1,0:T(8,128)(2,1)}, u32[]{:S(2)}, u32[]{:S(2)}) collective-permute-start(bf16[8,256,256]{2,1,0:T(8,128)(2,1)S(1)} %all_to_all.5), channel_id=1, source_target_pairs={{0,4},{4,0},{1,5},{5,1},{2,6},{6,2},{3,7},{7,3},{8,12},{12,8},{9,1... | collective-permute-start | bytes 3145736 | tf_op jit(solution)/shard_map/ppermute | solution.py:263
  75.5 10.9 %collective-permute-start.5 = (bf16[8,256,256]{2,1,0:T(8,128)(2,1)S(1)}, bf16[8,256,256]{2,1,0:T(8,128)(2,1)}, u32[]{:S(2)}, u32[]{:S(2)}) collective-permute-start(bf16[8,256,256]{2,1,0:T(8,128)(2,1)S(1)} %collective-permute-done), channel_id=1, source_target_pairs={{0,4},{4,0},{1,5},{5,1},{2,6},{6,2},{3,7},{7,3},{8,12},{12,8},{9,1... | collective-permute-start | bytes 3145736 | tf_op jit(solution)/shard_map/ppermute | solution.py:263
  75.5 10.9 %collective-permute-start.6 = (bf16[8,256,256]{2,1,0:T(8,128)(2,1)S(1)}, bf16[8,256,256]{2,1,0:T(8,128)(2,1)}, u32[]{:S(2)}, u32[]{:S(2)}) collective-permute-start(bf16[8,256,256]{2,1,0:T(8,128)(2,1)S(1)} %collective-permute-done.1), channel_id=1, source_target_pairs={{0,4},{4,0},{1,5},{5,1},{2,6},{6,2},{3,7},{7,3},{8,12},{12,8},{9,1... | collective-permute-start | bytes 3145736 | tf_op jit(solution)/shard_map/ppermute | solution.py:263
  79.6 6.0 %collective-permute-start.7 = (bf16[8,128,256]{2,1,0:T(8,128)(2,1)}, bf16[8,128,256]{2,1,0:T(8,128)(2,1)S(1)}, u32[]{:S(2)}, u32[]{:S(2)}) collective-permute-start(bf16[8,128,256]{2,1,0:T(8,128)(2,1)} %collective-permute-done.2.refs_7_), channel_id=1, source_target_pairs={{0,4},{4,0},{1,5},{5,1},{2,6},{6,2},{3,7},{7,3},{8,12},{12,8},{9,1... | collective-permute-start | bytes 1572872 | tf_op jit(solution)/shard_map/ppermute | solution.py:263
  83.9 2.5 %collective-permute-start.8 = (bf16[8,128,256]{2,1,0:T(8,128)(2,1)}, bf16[8,128,256]{2,1,0:T(8,128)(2,1)S(1)}, u32[]{:S(2)}, u32[]{:S(2)}) collective-permute-start(bf16[8,128,256]{2,1,0:T(8,128)(2,1)} %collective-permute-done.3.refs_8_), channel_id=1, source_target_pairs={{0,4},{4,0},{1,5},{5,1},{2,6},{6,2},{3,7},{7,3},{8,12},{12,8},{9,1... | collective-permute-start | bytes 1572872 | tf_op jit(solution)/shard_map/ppermute | solution.py:263
  103.3 7.6 %collective-permute-start.9 = (bf16[4,8,256,256]{3,2,1,0:T(8,128)(2,1)}, bf16[4,8,256,256]{3,2,1,0:T(8,128)(2,1)}, u32[]{:S(2)}, u32[]{:S(2)}) collective-permute-start(bf16[4,8,256,256]{3,2,1,0:T(8,128)(2,1)} %bitcast.123), channel_id=1, source_target_pairs={{0,4},{4,0},{1,5},{5,1},{2,6},{6,2},{3,7},{7,3},{8,12},{12,8},{9,1... | collective-permute-start | bytes 12582920 | tf_op jit(solution)/shard_map/ppermute | solution.py:263
  108.5 7.8 %collective-permute-start.21 = (bf16[6,256,256]{2,1,0:T(8,128)(2,1)}, bf16[6,256,256]{2,1,0:T(8,128)(2,1)S(1)}, u32[]{:S(2)}, u32[]{:S(2)}) collective-permute-start(bf16[6,256,256]{2,1,0:T(8,128)(2,1)} %get-tuple-element.55), channel_id=1, source_target_pairs={{0,4},{4,0},{1,5},{5,1},{2,6},{6,2},{3,7},{7,3},{8,12},{12,8},{9,1... | collective-permute-start | bytes 2359304 | tf_op jit(solution)/shard_map/ppermute | solution.py:263
  113.5 14.0 %collective-permute-start.11 = (bf16[8,128,256]{2,1,0:T(8,128)(2,1)}, bf16[8,128,256]{2,1,0:T(8,128)(2,1)S(1)}, u32[]{:S(2)}, u32[]{:S(2)}) collective-permute-start(bf16[8,128,256]{2,1,0:T(8,128)(2,1)} %get-tuple-element.66), channel_id=1, source_target_pairs={{0,24},{8,0},{16,8},{24,16},{1,25},{9,1},{17,9},{25,17},{2,26},{10... | collective-permute-start | bytes 1572872 | tf_op jit(solution)/shard_map/ppermute | solution.py:263
  116.3 14.0 %collective-permute-start.10 = (bf16[8,128,256]{2,1,0:T(8,128)(2,1)S(1)}, bf16[8,128,256]{2,1,0:T(8,128)(2,1)S(1)}, u32[]{:S(2)}, u32[]{:S(2)}) collective-permute-start(bf16[8,128,256]{2,1,0:T(8,128)(2,1)S(1)} %get-tuple-element.67), channel_id=1, source_target_pairs={{0,8},{8,16},{16,24},{24,0},{1,9},{9,17},{17,25},{25,1},{2,10},{10... | collective-permute-start | bytes 1572872 | tf_op jit(solution)/shard_map/ppermute | solution.py:263
  116.6 21.6 %collective-permute-start.22 = (bf16[384,256]{1,0:T(8,128)(2,1)S(1)}, bf16[384,256]{1,0:T(8,128)(2,1)S(1)}, u32[]{:S(2)}, u32[]{:S(2)}) collective-permute-start(bf16[384,256]{1,0:T(8,128)(2,1)S(1)} %get-tuple-element.81), channel_id=1, source_target_pairs={{0,8},{8,16},{16,24},{24,0},{1,9},{9,17},{17,25},{25,1},{2,10},{10... | collective-permute-start | bytes 589832 | tf_op jit(solution)/shard_map/ppermute | solution.py:263
  116.6 21.5 %collective-permute-start.23 = (bf16[384,256]{1,0:T(8,128)(2,1)S(1)}, bf16[384,256]{1,0:T(8,128)(2,1)S(1)}, u32[]{:S(2)}, u32[]{:S(2)}) collective-permute-start(bf16[384,256]{1,0:T(8,128)(2,1)S(1)} %get-tuple-element.83), channel_id=1, source_target_pairs={{0,24},{8,0},{16,8},{24,16},{1,25},{9,1},{17,9},{25,17},{2,26},{10... | collective-permute-start | bytes 589832 | tf_op jit(solution)/shard_map/ppermute | solution.py:263
  119.4 18.7 %collective-permute-start.24 = (bf16[384,256]{1,0:T(8,128)(2,1)S(1)}, bf16[384,256]{1,0:T(8,128)(2,1)S(1)}, u32[]{:S(2)}, u32[]{:S(2)}) collective-permute-start(bf16[384,256]{1,0:T(8,128)(2,1)S(1)} %get-tuple-element.82), channel_id=1, source_target_pairs={{0,16},{8,24},{16,0},{24,8},{1,17},{9,25},{17,1},{25,9},{2,18},{10... | collective-permute-start | bytes 589832 | tf_op jit(solution)/shard_map/ppermute | solution.py:263
  134.2 23.5 %collective-permute-start.13 = (bf16[8,256,256]{2,1,0:T(8,128)(2,1)}, bf16[8,256,256]{2,1,0:T(8,128)(2,1)S(1)}, u32[]{:S(2)}, u32[]{:S(2)}) collective-permute-start(bf16[8,256,256]{2,1,0:T(8,128)(2,1)} %get-tuple-element.65), channel_id=1, source_target_pairs={{0,24},{8,0},{16,8},{24,16},{1,25},{9,1},{17,9},{25,17},{2,26},{10... | collective-permute-start | bytes 3145736 | tf_op jit(solution)/shard_map/ppermute | solution.py:263
  135.0 25.5 %collective-permute-start.12 = (bf16[8,256,256]{2,1,0:T(8,128)(2,1)S(1)}, bf16[8,256,256]{2,1,0:T(8,128)(2,1)S(1)}, u32[]{:S(2)}, u32[]{:S(2)}) collective-permute-start(bf16[8,256,256]{2,1,0:T(8,128)(2,1)S(1)} %get-tuple-element.64), channel_id=1, source_target_pairs={{0,8},{8,16},{16,24},{24,0},{1,9},{9,17},{17,25},{25,1},{2,10},{10... | collective-permute-start | bytes 3145736 | tf_op jit(solution)/shard_map/ppermute | solution.py:263
  138.2 4.9 %collective-permute-start.25 = (bf16[384,256]{1,0:T(8,128)(2,1)S(1)}, bf16[384,256]{1,0:T(8,128)(2,1)S(1)}, u32[]{:S(2)}, u32[]{:S(2)}) collective-permute-start(bf16[384,256]{1,0:T(8,128)(2,1)S(1)} %fusion.29), channel_id=1, source_target_pairs={{0,32},{32,0},{64,96},{96,64},{128,160},{160,128},{192,224},{224,1... | collective-permute-start | bytes 589832 | tf_op jit(solution)/shard_map/ppermute | solution.py:291
  143.9 10.2 %collective-permute-start.26 = (bf16[384,256]{1,0:T(8,128)(2,1)}, bf16[384,256]{1,0:T(8,128)(2,1)}, u32[]{:S(2)}, u32[]{:S(2)}) collective-permute-start(bf16[384,256]{1,0:T(8,128)(2,1)} %add_convert_fusion.7), channel_id=1, source_target_pairs={{0,64},{32,96},{64,0},{96,32},{128,192},{160,224},{192,128},{224,1... | collective-permute-start | bytes 589832 | tf_op jit(solution)/shard_map/ppermute | solution.py:291
  155.1 16.9 %collective-permute-start.27 = (bf16[384,256]{1,0:T(8,128)(2,1)S(1)}, bf16[384,256]{1,0:T(8,128)(2,1)S(1)}, u32[]{:S(2)}, u32[]{:S(2)}) collective-permute-start(bf16[384,256]{1,0:T(8,128)(2,1)S(1)} %add_convert_fusion.6), channel_id=1, source_target_pairs={{0,128},{32,160},{64,192},{96,224},{128,0},{160,32},{192,64},{224,... | collective-permute-start | bytes 589832 | tf_op jit(solution)/shard_map/ppermute | solution.py:291
  162.6 10.6 %collective-permute-start.14 = (bf16[256,256]{1,0:T(8,128)(2,1)S(1)}, bf16[256,256]{1,0:T(8,128)(2,1)S(1)}, u32[]{:S(2)}, u32[]{:S(2)}) collective-permute-start(bf16[256,256]{1,0:T(8,128)(2,1)S(1)} %get-tuple-element.76), channel_id=1, source_target_pairs={{0,128},{32,160},{64,192},{96,224},{128,0},{160,32},{192,64},{224,... | collective-permute-start | bytes 393224 | tf_op jit(solution)/shard_map/ppermute | solution.py:263
  165.1 21.5 %collective-permute-start.15 = (bf16[256,256]{1,0:T(8,128)(2,1)S(1)}, bf16[256,256]{1,0:T(8,128)(2,1)S(1)}, u32[]{:S(2)}, u32[]{:S(2)}) collective-permute-start(bf16[256,256]{1,0:T(8,128)(2,1)S(1)} %get-tuple-element.75), channel_id=1, source_target_pairs={{0,96},{32,128},{64,160},{96,192},{128,224},{160,0},{192,32},{224,... | collective-permute-start | bytes 393224 | tf_op jit(solution)/shard_map/ppermute | solution.py:263
  165.3 24.2 %collective-permute-start.16 = (bf16[256,256]{1,0:T(8,128)(2,1)S(1)}, bf16[256,256]{1,0:T(8,128)(2,1)S(1)}, u32[]{:S(2)}, u32[]{:S(2)}) collective-permute-start(bf16[256,256]{1,0:T(8,128)(2,1)S(1)} %get-tuple-element.74), channel_id=1, source_target_pairs={{0,160},{32,192},{64,224},{96,0},{128,32},{160,64},{192,96},{224,1... | collective-permute-start | bytes 393224 | tf_op jit(solution)/shard_map/ppermute | solution.py:263
  169.6 19.9 %collective-permute-start.17 = (bf16[256,256]{1,0:T(8,128)(2,1)S(1)}, bf16[256,256]{1,0:T(8,128)(2,1)S(1)}, u32[]{:S(2)}, u32[]{:S(2)}) collective-permute-start(bf16[256,256]{1,0:T(8,128)(2,1)S(1)} %get-tuple-element.73), channel_id=1, source_target_pairs={{0,64},{32,96},{64,128},{96,160},{128,192},{160,224},{192,0},{224,... | collective-permute-start | bytes 393224 | tf_op jit(solution)/shard_map/ppermute | solution.py:263
  172.0 17.6 %collective-permute-start.18 = (bf16[256,256]{1,0:T(8,128)(2,1)S(1)}, bf16[256,256]{1,0:T(8,128)(2,1)S(1)}, u32[]{:S(2)}, u32[]{:S(2)}) collective-permute-start(bf16[256,256]{1,0:T(8,128)(2,1)S(1)} %get-tuple-element.72), channel_id=1, source_target_pairs={{0,192},{32,224},{64,0},{96,32},{128,64},{160,96},{192,128},{224,1... | collective-permute-start | bytes 393224 | tf_op jit(solution)/shard_map/ppermute | solution.py:263
  173.3 22.8 %collective-permute-start.28 = (bf16[384,256]{1,0:T(8,128)(2,1)S(1)}, bf16[384,256]{1,0:T(8,128)(2,1)S(1)}, u32[]{:S(2)}, u32[]{:S(2)}) collective-permute-start(bf16[384,256]{1,0:T(8,128)(2,1)S(1)} %add_convert_fusion.4), channel_id=1, source_target_pairs={{0,8},{8,16},{16,24},{24,0},{1,9},{9,17},{17,25},{25,1},{2,10},{10... | collective-permute-start | bytes 589832 | tf_op jit(solution)/shard_map/ppermute | solution.py:263
  186.6 9.5 %collective-permute-start.29 = (bf16[384,256]{1,0:T(8,128)(2,1)S(1)}, bf16[384,256]{1,0:T(8,128)(2,1)S(1)}, u32[]{:S(2)}, u32[]{:S(2)}) collective-permute-start(bf16[384,256]{1,0:T(8,128)(2,1)S(1)} %add_convert_fusion.4), channel_id=1, source_target_pairs={{0,16},{8,24},{16,0},{24,8},{1,17},{9,25},{17,1},{25,9},{2,18},{10... | collective-permute-start | bytes 589832 | tf_op jit(solution)/shard_map/ppermute | solution.py:263
  189.5 7.8 %collective-permute-start.30 = (bf16[384,256]{1,0:T(8,128)(2,1)S(1)}, bf16[384,256]{1,0:T(8,128)(2,1)S(1)}, u32[]{:S(2)}, u32[]{:S(2)}) collective-permute-start(bf16[384,256]{1,0:T(8,128)(2,1)S(1)} %add_convert_fusion.4), channel_id=1, source_target_pairs={{0,24},{8,0},{16,8},{24,16},{1,25},{9,1},{17,9},{25,17},{2,26},{10... | collective-permute-start | bytes 589832 | tf_op jit(solution)/shard_map/ppermute | solution.py:263
  189.5 5.4 %collective-permute-start.19 = (bf16[256,256]{1,0:T(8,128)(2,1)S(1)}, bf16[256,256]{1,0:T(8,128)(2,1)S(1)}, u32[]{:S(2)}, u32[]{:S(2)}) collective-permute-start(bf16[256,256]{1,0:T(8,128)(2,1)S(1)} %get-tuple-element.71), channel_id=1, source_target_pairs={{0,32},{32,64},{64,96},{96,128},{128,160},{160,192},{192,224},{224... | collective-permute-start | bytes 393224 | tf_op jit(solution)/shard_map/ppermute | solution.py:263
  189.6 5.3 %collective-permute-start.20 = (bf16[256,256]{1,0:T(8,128)(2,1)S(1)}, bf16[256,256]{1,0:T(8,128)(2,1)S(1)}, u32[]{:S(2)}, u32[]{:S(2)}) collective-permute-start(bf16[256,256]{1,0:T(8,128)(2,1)S(1)} %get-tuple-element.70), channel_id=1, source_target_pairs={{0,224},{32,0},{64,32},{96,64},{128,96},{160,128},{192,160},{224,1... | collective-permute-start | bytes 393224 | tf_op jit(solution)/shard_map/ppermute | solution.py:263
  197.7 3.5 %collective-permute-start.31 = (bf16[6,256,256]{2,1,0:T(8,128)(2,1)S(1)}, bf16[6,256,256]{2,1,0:T(8,128)(2,1)S(1)}, u32[]{:S(2)}, u32[]{:S(2)}) collective-permute-start(bf16[6,256,256]{2,1,0:T(8,128)(2,1)S(1)} %bitcast.113), channel_id=1, source_target_pairs={{0,4},{4,0},{1,5},{5,1},{2,6},{6,2},{3,7},{7,3},{8,12},{12,8},{9,1... | collective-permute-start | bytes 2359304 | tf_op jit(solution)/shard_map/ppermute | solution.py:263
  (14 other events, 199.2 us)

commit v2 on v1

--- a/solution.py
+++ b/solution.py
@@ -280,8 +280,8 @@
     left = shift(row, "x", 1)
     right = shift(row, "x", -1)
     left, right, *made = lax.optimization_barrier((left, right, *made))
-    far_low = shift(left[:, :128], "x", 1)
-    far_high = shift(right[:, 128:], "x", -1)
+    far_low = shift(left[: z_size // 2], "x", 1)
+    far_high = shift(right[z_size // 2 :], "x", -1)
     mine = [row, left, right, far_low, far_high]
     return mine + [shift(v, "c", 1) for v in mine], made
 
@@ -344,7 +344,6 @@
         shares.append(shift(pick(head, 0, (x_id + by) % x_size), "x", by))
     head = add(*shares).astype(BF)
     head = add(head, pair(head, "z", 1)).astype(BF)
-    head = after(head, firsts[-1][1])
     head = add(head, pair(head, "z", 2)).astype(BF)
     head = add(head, pair(head, "z", 4)).astype(BF)
     head = after(head, seconds[0][1])
@@ -366,10 +365,11 @@
     other_core = (owner % c_size != c_id).astype(jnp.int32)
     dx = (owner_x - x_id) % x_size
     dz = (owner_z - z_id) % z_size
+    upper = (owner_z >= z_size // 2).astype(jnp.int32)
     bank = jnp.where(
-        dx == 0, 0, jnp.where(dx == 3, 1, jnp.where(dx == 1, 2, 3 + block))
+        dx == 0, 0, jnp.where(dx == 3, 1, jnp.where(dx == 1, 2, 3 + upper))
     ) + 5 * other_core
-    bank_row = jnp.where(dx == 2, owner_z, 2 * owner_z + block)
+    bank_row = 2 * (owner_z - jnp.where(dx == 2, upper * (z_size // 2), 0)) + block
     position = jnp.where(dz == 0, 7, jnp.where(dz == 4, 0, jnp.where(dz < 4, 7 - 2 * dz, 2 * dz - 8)))
     place = 2 * (dx * z_size + position) + block
     place = place + 2 * x_size * z_size * other_core

time: 204 us -> 203 us (level)
  waiting for transfers between devices: 63.4 us -> 65.9 us
    ppermute x3, waiting for transfers between devices: 13.1 us -> 16.1 us  [pair(): return lax.ppermute(values, axis, [(i, i ^ bit) for i in range(size)])]
  transfers between devices with their start and end apart: 32 -> 32, of which waited for: 15 -> 16; matrix products, arithmetic and copies ran while one was open for 9% -> 8% of each run, Pallas kernels for 6% -> 6%
where the time goes in v2:
time: 203 us; the launch traced here: 202 us
  waiting for transfers between devices  65.9 us (32%)
  starting transfers between devices  42.6 us (21%)
  blocking collectives  36.1 us (18%)
  Pallas kernels  27.7 us (14%)
  other arithmetic  16 us (8%)
  matrix products  6.78 us (3%)
  local copies, waits for them, and re-layouts  5.01 us (2%)
  between operations  2.25 us (1%)
    ppermute x29, waiting for transfers between devices, shift(): lax.ppermute(values, axis, [(i, (i + by) % size) for i in range(size)])  49.8 us
    ppermute x29, starting transfers between devices, shift(): lax.ppermute(values, axis, [(i, (i + by) % size) for i in range(size)])  39.6 us
    all_to_all x1, blocking collectives, exchange(): return lax.all_to_all(values, axis, 0, 0, tiled=True)  36.1 us
    pallas_call x1, Pallas kernels, score(): pl.pallas_call(lambda *refs: score_kernel(*refs, per_group=per_group, ban...  16.2 us
    ppermute x3, waiting for transfers between devices, pair(): return lax.ppermute(values, axis, [(i, i ^ bit) for i in range(size)])  16.1 us
    pallas_call x1, Pallas kernels, make_queries(): pl.pallas_call(lambda *refs: query_kernel(*refs, groups=groups), out_shap...  6.73 us
    pallas_call x1, Pallas kernels, head_product(): pl.pallas_call(head_kernel, out_shape=(half, half, jax.ShapeDtypeStruct((...  4.76 us
  transfers between devices with their start and end apart: 32, of which 16 were waited for; matrix products, arithmetic and copies ran while one was open for 8% of the time, Pallas kernels for 6%

profile of v2, /device:TPU:1, one launch (start us, length us, event | category | flops | bytes accessed | tf_op | source)
XLA Modules:
  0.0 202.3 jit_solution(5342604987760586217)
XLA Ops:
  1.9 3.1 %fusion.5 = bf16[1024,256]{1,0:T(8,128)(2,1)S(1)} fusion(bf16[1024,5]{1,0:T(8,128)(2,1)S(1)} %reshape_reshape.3, bf16[5,256]{1,0:T(8,128)(2,1)} %param.9), kind=kOutput, calls=%fused_computation.12 | convolution fusion | flops 19660800 | bytes 537088 | tf_op jit(solution)/shard_map/dot_general | solution.py:24
  7.7 36.1 %all_to_all.5 = bf16[8,256,256]{2,1,0:T(8,128)(2,1)S(1)} all-to-all(bf16[8,256,256]{2,1,0:T(8,128)(2,1)S(1)} %broadcast_in_dim.14), channel_id=1, replica_groups=mesh['z'=8,'x'=4,'c'=2,'rep'=4] {'z'}, dimensions={0} | all-to-all | bytes 2097152 | tf_op jit(solution)/shard_map/all_to_all | solution.py:267
  48.6 6.7 %queries.1 = (bf16[8,384,256]{2,1,0:T(8,128)(2,1)}, bf16[8,384,256]{2,1,0:T(8,128)(2,1)}, f32[8,384,3]{2,1,0:T(8,128)}) custom-call(bf16[256,256]{1,0:T(8,128)(2,1)} %copy-done.4, bf16[256,256]{1,0:T(8,128)(2,1)} %fusion.38.refs_1_.ctx_ref, bf16[12,256,256]{2,1,0:T(8,128)(2,1)} %bitcast.120), custom_call_target="tpu_custom_call" | custom-call | tf_op jit(solution)/shard_map/queries/pallas_call | solution.py:195
  55.3 11.8 %collective-permute-done = bf16[8,256,256]{2,1,0:T(8,128)(2,1)S(1)} collective-permute-done((bf16[8,256,256]{2,1,0:T(8,128)(2,1)S(1)}, bf16[8,256,256]{2,1,0:T(8,128)(2,1)S(1)}, u32[]{:S(2)}, u32[]{:S(2)}) %collective-permute-start) | collective-permute-done | bytes 1048608 | tf_op jit(solution)/shard_map/ppermute | solution.py:263
  69.8 1.7 collective-permute-start.3
  71.6 3.9 %collective-permute-start.4 = (bf16[8,256,256]{2,1,0:T(8,128)(2,1)S(1)}, bf16[8,256,256]{2,1,0:T(8,128)(2,1)}, u32[]{:S(2)}, u32[]{:S(2)}) collective-permute-start(bf16[8,256,256]{2,1,0:T(8,128)(2,1)S(1)} %all_to_all.5), channel_id=1, source_target_pairs={{0,4},{4,0},{1,5},{5,1},{2,6},{6,2},{3,7},{7,3},{8,12},{12,8},{9,1... | collective-permute-start | bytes 3145736 | tf_op jit(solution)/shard_map/ppermute | solution.py:263
  76.3 3.3 %collective-permute-done.2 = bf16[4,256,256]{2,1,0:T(8,128)(2,1)} collective-permute-done((bf16[4,256,256]{2,1,0:T(8,128)(2,1)}, bf16[4,256,256]{2,1,0:T(8,128)(2,1)}, u32[]{:S(2)}, u32[]{:S(2)}) %collective-permute-start.2) | collective-permute-done | bytes 524320 | tf_op jit(solution)/shard_map/ppermute | solution.py:263
  79.6 4.3 %collective-permute-start.7 = (bf16[4,256,256]{2,1,0:T(8,128)(2,1)}, bf16[4,256,256]{2,1,0:T(8,128)(2,1)S(1)}, u32[]{:S(2)}, u32[]{:S(2)}) collective-permute-start(bf16[4,256,256]{2,1,0:T(8,128)(2,1)} %collective-permute-done.2), channel_id=1, source_target_pairs={{0,4},{4,0},{1,5},{5,1},{2,6},{6,2},{3,7},{7,3},{8,12},{12,8},{9,1... | collective-permute-start | bytes 1572872 | tf_op jit(solution)/shard_map/ppermute | solution.py:263
  87.2 16.2 %score.1 = (bf16[64,128,256]{2,1,0:T(8,128)(2,1)}, bf16[64,128,256]{2,1,0:T(8,128)(2,1)}, bf16[12,256,256]{2,1,0:T(8,128)(2,1)}, bf16[12,256,256]{2,1,0:T(8,128)(2,1)}) custom-call(s32[3,32]{1,0:T(4,128)} %pad_add_fusion.refs_0_, bf16[8,384,256]{2,1,0:T(8,128)(2,1)} %get-tuple-element.32.refs_1_, bf16[8,384,256]{2,1,0:T(8,128)(2,1)} %get-tuple-element.33.refs_2_, ...), custom_call_target="tpu_custom_call" | custom-call | tf_op jit(solution)/shard_map/score/pallas_call | solution.py:220
  103.9 4.8 %heads.1 = (bf16[6,256,256]{2,1,0:T(8,128)(2,1)}, bf16[6,256,256]{2,1,0:T(8,128)(2,1)}, f32[256,256]{1,0:T(8,128)}) custom-call(s32[1]{0:T(128)} %bitcast.core_ref, bf16[256,256]{1,0:T(8,128)(2,1)} %fusion.38.refs_1_.ctx_ref, bf16[12,256,256]{2,1,0:T(8,128)(2,1)} %get-tuple-element.37.pg_ref, bf16[12,256,256]{2,1,0:T(8,128)(2,1)} %get-tuple-element.38.p_ref), custom_call_target="tpu_custom_call" | custom-call | tf_op jit(solution)/shard_map/heads/pallas_call | solution.py:251
  108.8 2.2 %collective-permute-done.9 = bf16[4,8,256,256]{3,2,1,0:T(8,128)(2,1)} collective-permute-done((bf16[4,8,256,256]{3,2,1,0:T(8,128)(2,1)}, bf16[4,8,256,256]{3,2,1,0:T(8,128)(2,1)}, u32[]{:S(2)}, u32[]{:S(2)}) %collective-permute-start.9) | collective-permute-done | bytes 4194336 | tf_op jit(solution)/shard_map/ppermute | solution.py:263
  111.1 2.7 %fusion.17 = (bf16[8,128,256]{2,1,0:T(8,128)(2,1)S(1)}, bf16[8,128,256]{2,1,0:T(8,128)(2,1)}) fusion(bf16[4,8,256,256]{3,2,1,0:T(8,128)(2,1)} %collective-permute-done.9, bf16[4,8,256,256]{3,2,1,0:T(8,128)(2,1)} %bitcast.109), kind=kLoop, calls=%fused_computation.38 | loop fusion | flops 2097152 | bytes 3145728 | tf_op jit(solution)/shard_map/convert_element_type | solution.py:320
  114.5 2.0 collective-permute-start.11
  116.8 2.7 %collective-permute-start.23 = (bf16[384,256]{1,0:T(8,128)(2,1)S(1)}, bf16[384,256]{1,0:T(8,128)(2,1)S(1)}, u32[]{:S(2)}, u32[]{:S(2)}) collective-permute-start(bf16[384,256]{1,0:T(8,128)(2,1)S(1)} %get-tuple-element.82), channel_id=1, source_target_pairs={{0,24},{8,0},{16,8},{24,16},{1,25},{9,1},{17,9},{25,17},{2,26},{10... | collective-permute-start | bytes 589832 | tf_op jit(solution)/shard_map/ppermute | solution.py:263
  119.5 9.0 %collective-permute-done.10 = bf16[8,128,256]{2,1,0:T(8,128)(2,1)S(1)} collective-permute-done((bf16[8,128,256]{2,1,0:T(8,128)(2,1)}, bf16[8,128,256]{2,1,0:T(8,128)(2,1)S(1)}, u32[]{:S(2)}, u32[]{:S(2)}) %collective-permute-start.10) | collective-permute-done | bytes 524320 | tf_op jit(solution)/shard_map/ppermute | solution.py:263
  128.5 3.9 %fusion.1 = (bf16[8,256,256]{2,1,0:T(8,128)(2,1)S(1)}, bf16[8,256,256]{2,1,0:T(8,128)(2,1)}) fusion(bf16[8,128,256]{2,1,0:T(8,128)(2,1)S(1)} %collective-permute-done.10, bf16[4,8,256,256]{3,2,1,0:T(8,128)(2,1)} %collective-permute-done.9, bf16[4,8,256,256]{3,2,1,0:T(8,128)(2,1)} %bitcast.110, bf16[8,128,256]{2,1,0:T(8,128)(2,1)S(1)} %collective-permute-done.11), kind=kLoop, calls=%fused_computation.4 | loop fusion | flops 6291456 | bytes 7340032 | tf_op jit(solution)/shard_map/convert_element_type | solution.py:328
  132.4 2.1 %collective-permute-start.13 = (bf16[8,256,256]{2,1,0:T(8,128)(2,1)}, bf16[8,256,256]{2,1,0:T(8,128)(2,1)S(1)}, u32[]{:S(2)}, u32[]{:S(2)}) collective-permute-start(bf16[8,256,256]{2,1,0:T(8,128)(2,1)} %get-tuple-element.64), channel_id=1, source_target_pairs={{0,24},{8,0},{16,8},{24,16},{1,25},{9,1},{17,9},{25,17},{2,26},{10... | collective-permute-start | bytes 3145736 | tf_op jit(solution)/shard_map/ppermute | solution.py:263
  134.6 3.4 %collective-permute-done.24 = bf16[384,256]{1,0:T(8,128)(2,1)S(1)} collective-permute-done((bf16[384,256]{1,0:T(8,128)(2,1)S(1)}, bf16[384,256]{1,0:T(8,128)(2,1)S(1)}, u32[]{:S(2)}, u32[]{:S(2)}) %collective-permute-start.24) | collective-permute-done | bytes 196640 | tf_op jit(solution)/shard_map/ppermute | solution.py:263
  138.2 4.8 %collective-permute-done.25 = bf16[384,256]{1,0:T(8,128)(2,1)S(1)} collective-permute-done((bf16[384,256]{1,0:T(8,128)(2,1)S(1)}, bf16[384,256]{1,0:T(8,128)(2,1)S(1)}, u32[]{:S(2)}, u32[]{:S(2)}) %collective-permute-start.25) | collective-permute-done | bytes 196640 | tf_op jit(solution)/shard_map/ppermute | solution.py:291
  143.9 10.8 %collective-permute-done.26 = bf16[384,256]{1,0:T(8,128)(2,1)} collective-permute-done((bf16[384,256]{1,0:T(8,128)(2,1)}, bf16[384,256]{1,0:T(8,128)(2,1)}, u32[]{:S(2)}, u32[]{:S(2)}) %collective-permute-start.26) | collective-permute-done | bytes 196640 | tf_op jit(solution)/shard_map/ppermute | solution.py:291
  155.8 2.8 %collective-permute-start.27 = (bf16[384,256]{1,0:T(8,128)(2,1)S(1)}, bf16[384,256]{1,0:T(8,128)(2,1)S(1)}, u32[]{:S(2)}, u32[]{:S(2)}) collective-permute-start(bf16[384,256]{1,0:T(8,128)(2,1)S(1)} %add_convert_fusion.6), channel_id=1, source_target_pairs={{0,128},{32,160},{64,192},{96,224},{128,0},{160,32},{192,64},{224,... | collective-permute-start | bytes 589832 | tf_op jit(solution)/shard_map/ppermute | solution.py:291
  158.8 2.1 %fusion.94 = (bf16[8,256,256]{2,1,0:T(8,128)(2,1)S(1)}, f32[8,256,256]{2,1,0:T(8,128)S(1)}) fusion(bf16[8,256,256]{2,1,0:T(8,128)(2,1)S(1)} %collective-permute-done.13, bf16[8,256,256]{2,1,0:T(8,128)(2,1)S(1)} %collective-permute-done.12, bf16[4,8,256,256]{3,2,1,0:T(8,128)(2,1)} %collective-permute-done.9, bf16[4,8,256,256]{3,2,1,0:T(8,128)(2,1)} %bitcast.111), kind=kLoop, calls=%fused_computation.192 | loop fusion | flops 4194304 | bytes 7340032 | tf_op jit(solution)/shard_map/convert.7
  160.9 2.5 %collective-permute-start.14 = (bf16[256,256]{1,0:T(8,128)(2,1)S(1)}, bf16[256,256]{1,0:T(8,128)(2,1)S(1)}, u32[]{:S(2)}, u32[]{:S(2)}) collective-permute-start(bf16[256,256]{1,0:T(8,128)(2,1)S(1)} %get-tuple-element.75), channel_id=1, source_target_pairs={{0,128},{32,160},{64,192},{96,224},{128,0},{160,32},{192,64},{224,... | collective-permute-start | bytes 393224 | tf_op jit(solution)/shard_map/ppermute | solution.py:263
  164.8 3.2 %collective-permute-start.16 = (bf16[256,256]{1,0:T(8,128)(2,1)S(1)}, bf16[256,256]{1,0:T(8,128)(2,1)S(1)}, u32[]{:S(2)}, u32[]{:S(2)}) collective-permute-start(bf16[256,256]{1,0:T(8,128)(2,1)S(1)} %get-tuple-element.73), channel_id=1, source_target_pairs={{0,160},{32,192},{64,224},{96,0},{128,32},{160,64},{192,96},{224,1... | collective-permute-start | bytes 393224 | tf_op jit(solution)/shard_map/ppermute | solution.py:263
  167.9 2.3 %collective-permute-start.17 = (bf16[256,256]{1,0:T(8,128)(2,1)S(1)}, bf16[256,256]{1,0:T(8,128)(2,1)S(1)}, u32[]{:S(2)}, u32[]{:S(2)}) collective-permute-start(bf16[256,256]{1,0:T(8,128)(2,1)S(1)} %get-tuple-element.72), channel_id=1, source_target_pairs={{0,64},{32,96},{64,128},{96,160},{128,192},{160,224},{192,0},{224,... | collective-permute-start | bytes 393224 | tf_op jit(solution)/shard_map/ppermute | solution.py:263
  172.8 2.0 collective-permute-done.14
  174.9 12.4 %collective-permute-done.15 = bf16[256,256]{1,0:T(8,128)(2,1)S(1)} collective-permute-done((bf16[256,256]{1,0:T(8,128)(2,1)S(1)}, bf16[256,256]{1,0:T(8,128)(2,1)S(1)}, u32[]{:S(2)}, u32[]{:S(2)}) %collective-permute-start.15) | collective-permute-done | bytes 131104 | tf_op jit(solution)/shard_map/ppermute | solution.py:263
  187.5 1.8 collective-permute-start.30
  189.9 2.1 %collective-permute-start.20 = (bf16[256,256]{1,0:T(8,128)(2,1)S(1)}, bf16[256,256]{1,0:T(8,128)(2,1)S(1)}, u32[]{:S(2)}, u32[]{:S(2)}) collective-permute-start(bf16[256,256]{1,0:T(8,128)(2,1)S(1)} %get-tuple-element.69), channel_id=1, source_target_pairs={{0,224},{32,0},{64,32},{96,64},{128,96},{160,128},{192,160},{224,1... | collective-permute-start | bytes 393224 | tf_op jit(solution)/shard_map/ppermute | solution.py:263
  192.1 2.6 %collective-permute-done.19 = bf16[256,256]{1,0:T(8,128)(2,1)S(1)} collective-permute-done((bf16[256,256]{1,0:T(8,128)(2,1)S(1)}, bf16[256,256]{1,0:T(8,128)(2,1)S(1)}, u32[]{:S(2)}, u32[]{:S(2)}) %collective-permute-start.19) | collective-permute-done | bytes 131104 | tf_op jit(solution)/shard_map/ppermute | solution.py:263
  196.7 1.7 collective-permute-start.31
  200.4 2.0 convert_multiply_fusion
  (108 shorter events, 27.0 us)
Async XLA Ops:
  43.7 23.4 %collective-permute-start = (bf16[8,256,256]{2,1,0:T(8,128)(2,1)S(1)}, bf16[8,256,256]{2,1,0:T(8,128)(2,1)S(1)}, u32[]{:S(2)}, u32[]{:S(2)}) collective-permute-start(bf16[8,256,256]{2,1,0:T(8,128)(2,1)S(1)} %all_to_all.5), channel_id=1, source_target_pairs={{0,8},{8,16},{16,24},{24,0},{1,9},{9,17},{17,25},{25,1},{2,10},{10... | collective-permute-start | bytes 3145736 | tf_op jit(solution)/shard_map/ppermute | solution.py:263
  44.9 22.2 %collective-permute-start.1 = (bf16[8,256,256]{2,1,0:T(8,128)(2,1)S(1)}, bf16[8,256,256]{2,1,0:T(8,128)(2,1)S(1)}, u32[]{:S(2)}, u32[]{:S(2)}) collective-permute-start(bf16[8,256,256]{2,1,0:T(8,128)(2,1)S(1)} %all_to_all.5), channel_id=1, source_target_pairs={{0,24},{8,0},{16,8},{24,16},{1,25},{9,1},{17,9},{25,17},{2,26},{10... | collective-permute-start | bytes 3145736 | tf_op jit(solution)/shard_map/ppermute | solution.py:263
  68.1 11.6 %collective-permute-start.2 = (bf16[4,256,256]{2,1,0:T(8,128)(2,1)}, bf16[4,256,256]{2,1,0:T(8,128)(2,1)}, u32[]{:S(2)}, u32[]{:S(2)}) collective-permute-start(bf16[4,256,256]{2,1,0:T(8,128)(2,1)} %slice.97), channel_id=1, source_target_pairs={{0,8},{8,16},{16,24},{24,0},{1,9},{9,17},{17,25},{25,1},{2,10},{10... | collective-permute-start | bytes 1572872 | tf_op jit(solution)/shard_map/ppermute | solution.py:263
  69.8 14.1 %collective-permute-start.3 = (bf16[4,256,256]{2,1,0:T(8,128)(2,1)}, bf16[4,256,256]{2,1,0:T(8,128)(2,1)}, u32[]{:S(2)}, u32[]{:S(2)}) collective-permute-start(bf16[4,256,256]{2,1,0:T(8,128)(2,1)} %slice.98), channel_id=1, source_target_pairs={{0,24},{8,0},{16,8},{24,16},{1,25},{9,1},{17,9},{25,17},{2,26},{10... | collective-permute-start | bytes 1572872 | tf_op jit(solution)/shard_map/ppermute | solution.py:263
  71.6 13.5 %collective-permute-start.4 = (bf16[8,256,256]{2,1,0:T(8,128)(2,1)S(1)}, bf16[8,256,256]{2,1,0:T(8,128)(2,1)}, u32[]{:S(2)}, u32[]{:S(2)}) collective-permute-start(bf16[8,256,256]{2,1,0:T(8,128)(2,1)S(1)} %all_to_all.5), channel_id=1, source_target_pairs={{0,4},{4,0},{1,5},{5,1},{2,6},{6,2},{3,7},{7,3},{8,12},{12,8},{9,1... | collective-permute-start | bytes 3145736 | tf_op jit(solution)/shard_map/ppermute | solution.py:263
  75.5 10.9 %collective-permute-start.5 = (bf16[8,256,256]{2,1,0:T(8,128)(2,1)S(1)}, bf16[8,256,256]{2,1,0:T(8,128)(2,1)}, u32[]{:S(2)}, u32[]{:S(2)}) collective-permute-start(bf16[8,256,256]{2,1,0:T(8,128)(2,1)S(1)} %collective-permute-done), channel_id=1, source_target_pairs={{0,4},{4,0},{1,5},{5,1},{2,6},{6,2},{3,7},{7,3},{8,12},{12,8},{9,1... | collective-permute-start | bytes 3145736 | tf_op jit(solution)/shard_map/ppermute | solution.py:263
  75.5 10.9 %collective-permute-start.6 = (bf16[8,256,256]{2,1,0:T(8,128)(2,1)S(1)}, bf16[8,256,256]{2,1,0:T(8,128)(2,1)}, u32[]{:S(2)}, u32[]{:S(2)}) collective-permute-start(bf16[8,256,256]{2,1,0:T(8,128)(2,1)S(1)} %collective-permute-done.1), channel_id=1, source_target_pairs={{0,4},{4,0},{1,5},{5,1},{2,6},{6,2},{3,7},{7,3},{8,12},{12,8},{9,1... | collective-permute-start | bytes 3145736 | tf_op jit(solution)/shard_map/ppermute | solution.py:263
  79.6 6.0 %collective-permute-start.7 = (bf16[4,256,256]{2,1,0:T(8,128)(2,1)}, bf16[4,256,256]{2,1,0:T(8,128)(2,1)S(1)}, u32[]{:S(2)}, u32[]{:S(2)}) collective-permute-start(bf16[4,256,256]{2,1,0:T(8,128)(2,1)} %collective-permute-done.2), channel_id=1, source_target_pairs={{0,4},{4,0},{1,5},{5,1},{2,6},{6,2},{3,7},{7,3},{8,12},{12,8},{9,1... | collective-permute-start | bytes 1572872 | tf_op jit(solution)/shard_map/ppermute | solution.py:263
  83.9 2.5 %collective-permute-start.8 = (bf16[4,256,256]{2,1,0:T(8,128)(2,1)}, bf16[4,256,256]{2,1,0:T(8,128)(2,1)S(1)}, u32[]{:S(2)}, u32[]{:S(2)}) collective-permute-start(bf16[4,256,256]{2,1,0:T(8,128)(2,1)} %collective-permute-done.3), channel_id=1, source_target_pairs={{0,4},{4,0},{1,5},{5,1},{2,6},{6,2},{3,7},{7,3},{8,12},{12,8},{9,1... | collective-permute-start | bytes 1572872 | tf_op jit(solution)/shard_map/ppermute | solution.py:263
  103.5 7.6 %collective-permute-start.9 = (bf16[4,8,256,256]{3,2,1,0:T(8,128)(2,1)}, bf16[4,8,256,256]{3,2,1,0:T(8,128)(2,1)}, u32[]{:S(2)}, u32[]{:S(2)}) collective-permute-start(bf16[4,8,256,256]{3,2,1,0:T(8,128)(2,1)} %bitcast.128), channel_id=1, source_target_pairs={{0,4},{4,0},{1,5},{5,1},{2,6},{6,2},{3,7},{7,3},{8,12},{12,8},{9,1... | collective-permute-start | bytes 12582920 | tf_op jit(solution)/shard_map/ppermute | solution.py:263
  108.7 7.8 %collective-permute-start.21 = (bf16[6,256,256]{2,1,0:T(8,128)(2,1)}, bf16[6,256,256]{2,1,0:T(8,128)(2,1)S(1)}, u32[]{:S(2)}, u32[]{:S(2)}) collective-permute-start(bf16[6,256,256]{2,1,0:T(8,128)(2,1)} %get-tuple-element.55), channel_id=1, source_target_pairs={{0,4},{4,0},{1,5},{5,1},{2,6},{6,2},{3,7},{7,3},{8,12},{12,8},{9,1... | collective-permute-start | bytes 2359304 | tf_op jit(solution)/shard_map/ppermute | solution.py:263
  113.7 14.7 %collective-permute-start.10 = (bf16[8,128,256]{2,1,0:T(8,128)(2,1)}, bf16[8,128,256]{2,1,0:T(8,128)(2,1)S(1)}, u32[]{:S(2)}, u32[]{:S(2)}) collective-permute-start(bf16[8,128,256]{2,1,0:T(8,128)(2,1)} %get-tuple-element.66), channel_id=1, source_target_pairs={{0,8},{8,16},{16,24},{24,0},{1,9},{9,17},{17,25},{25,1},{2,10},{10... | collective-permute-start | bytes 1572872 | tf_op jit(solution)/shard_map/ppermute | solution.py:263
  114.5 14.0 %collective-permute-start.11 = (bf16[8,128,256]{2,1,0:T(8,128)(2,1)S(1)}, bf16[8,128,256]{2,1,0:T(8,128)(2,1)S(1)}, u32[]{:S(2)}, u32[]{:S(2)}) collective-permute-start(bf16[8,128,256]{2,1,0:T(8,128)(2,1)S(1)} %get-tuple-element.65), channel_id=1, source_target_pairs={{0,24},{8,0},{16,8},{24,16},{1,25},{9,1},{17,9},{25,17},{2,26},{10... | collective-permute-start | bytes 1572872 | tf_op jit(solution)/shard_map/ppermute | solution.py:263
  116.7 17.8 %collective-permute-start.22 = (bf16[384,256]{1,0:T(8,128)(2,1)S(1)}, bf16[384,256]{1,0:T(8,128)(2,1)S(1)}, u32[]{:S(2)}, u32[]{:S(2)}) collective-permute-start(bf16[384,256]{1,0:T(8,128)(2,1)S(1)} %get-tuple-element.80), channel_id=1, source_target_pairs={{0,8},{8,16},{16,24},{24,0},{1,9},{9,17},{17,25},{25,1},{2,10},{10... | collective-permute-start | bytes 589832 | tf_op jit(solution)/shard_map/ppermute | solution.py:263
  116.8 17.7 %collective-permute-start.23 = (bf16[384,256]{1,0:T(8,128)(2,1)S(1)}, bf16[384,256]{1,0:T(8,128)(2,1)S(1)}, u32[]{:S(2)}, u32[]{:S(2)}) collective-permute-start(bf16[384,256]{1,0:T(8,128)(2,1)S(1)} %get-tuple-element.82), channel_id=1, source_target_pairs={{0,24},{8,0},{16,8},{24,16},{1,25},{9,1},{17,9},{25,17},{2,26},{10... | collective-permute-start | bytes 589832 | tf_op jit(solution)/shard_map/ppermute | solution.py:263
  119.5 18.5 %collective-permute-start.24 = (bf16[384,256]{1,0:T(8,128)(2,1)S(1)}, bf16[384,256]{1,0:T(8,128)(2,1)S(1)}, u32[]{:S(2)}, u32[]{:S(2)}) collective-permute-start(bf16[384,256]{1,0:T(8,128)(2,1)S(1)} %get-tuple-element.81), channel_id=1, source_target_pairs={{0,16},{8,24},{16,0},{24,8},{1,17},{9,25},{17,1},{25,9},{2,18},{10... | collective-permute-start | bytes 589832 | tf_op jit(solution)/shard_map/ppermute | solution.py:263
  132.4 26.2 %collective-permute-start.13 = (bf16[8,256,256]{2,1,0:T(8,128)(2,1)}, bf16[8,256,256]{2,1,0:T(8,128)(2,1)S(1)}, u32[]{:S(2)}, u32[]{:S(2)}) collective-permute-start(bf16[8,256,256]{2,1,0:T(8,128)(2,1)} %get-tuple-element.64), channel_id=1, source_target_pairs={{0,24},{8,0},{16,8},{24,16},{1,25},{9,1},{17,9},{25,17},{2,26},{10... | collective-permute-start | bytes 3145736 | tf_op jit(solution)/shard_map/ppermute | solution.py:263
  134.5 24.3 %collective-permute-start.12 = (bf16[8,256,256]{2,1,0:T(8,128)(2,1)S(1)}, bf16[8,256,256]{2,1,0:T(8,128)(2,1)S(1)}, u32[]{:S(2)}, u32[]{:S(2)}) collective-permute-start(bf16[8,256,256]{2,1,0:T(8,128)(2,1)S(1)} %get-tuple-element.63), channel_id=1, source_target_pairs={{0,8},{8,16},{16,24},{24,0},{1,9},{9,17},{17,25},{25,1},{2,10},{10... | collective-permute-start | bytes 3145736 | tf_op jit(solution)/shard_map/ppermute | solution.py:263
  138.1 4.9 %collective-permute-start.25 = (bf16[384,256]{1,0:T(8,128)(2,1)S(1)}, bf16[384,256]{1,0:T(8,128)(2,1)S(1)}, u32[]{:S(2)}, u32[]{:S(2)}) collective-permute-start(bf16[384,256]{1,0:T(8,128)(2,1)S(1)} %fusion.29), channel_id=1, source_target_pairs={{0,32},{32,0},{64,96},{96,64},{128,160},{160,128},{192,224},{224,1... | collective-permute-start | bytes 589832 | tf_op jit(solution)/shard_map/ppermute | solution.py:291
  143.7 11.0 %collective-permute-start.26 = (bf16[384,256]{1,0:T(8,128)(2,1)}, bf16[384,256]{1,0:T(8,128)(2,1)}, u32[]{:S(2)}, u32[]{:S(2)}) collective-permute-start(bf16[384,256]{1,0:T(8,128)(2,1)} %add_convert_fusion.7), channel_id=1, source_target_pairs={{0,64},{32,96},{64,0},{96,32},{128,192},{160,224},{192,128},{224,1... | collective-permute-start | bytes 589832 | tf_op jit(solution)/shard_map/ppermute | solution.py:291
  155.8 16.1 %collective-permute-start.27 = (bf16[384,256]{1,0:T(8,128)(2,1)S(1)}, bf16[384,256]{1,0:T(8,128)(2,1)S(1)}, u32[]{:S(2)}, u32[]{:S(2)}) collective-permute-start(bf16[384,256]{1,0:T(8,128)(2,1)S(1)} %add_convert_fusion.6), channel_id=1, source_target_pairs={{0,128},{32,160},{64,192},{96,224},{128,0},{160,32},{192,64},{224,... | collective-permute-start | bytes 589832 | tf_op jit(solution)/shard_map/ppermute | solution.py:291
  160.9 13.9 %collective-permute-start.14 = (bf16[256,256]{1,0:T(8,128)(2,1)S(1)}, bf16[256,256]{1,0:T(8,128)(2,1)S(1)}, u32[]{:S(2)}, u32[]{:S(2)}) collective-permute-start(bf16[256,256]{1,0:T(8,128)(2,1)S(1)} %get-tuple-element.75), channel_id=1, source_target_pairs={{0,128},{32,160},{64,192},{96,224},{128,0},{160,32},{192,64},{224,... | collective-permute-start | bytes 393224 | tf_op jit(solution)/shard_map/ppermute | solution.py:263
  163.5 23.9 %collective-permute-start.15 = (bf16[256,256]{1,0:T(8,128)(2,1)S(1)}, bf16[256,256]{1,0:T(8,128)(2,1)S(1)}, u32[]{:S(2)}, u32[]{:S(2)}) collective-permute-start(bf16[256,256]{1,0:T(8,128)(2,1)S(1)} %get-tuple-element.74), channel_id=1, source_target_pairs={{0,96},{32,128},{64,160},{96,192},{128,224},{160,0},{192,32},{224,... | collective-permute-start | bytes 393224 | tf_op jit(solution)/shard_map/ppermute | solution.py:263
  164.8 22.7 %collective-permute-start.16 = (bf16[256,256]{1,0:T(8,128)(2,1)S(1)}, bf16[256,256]{1,0:T(8,128)(2,1)S(1)}, u32[]{:S(2)}, u32[]{:S(2)}) collective-permute-start(bf16[256,256]{1,0:T(8,128)(2,1)S(1)} %get-tuple-element.73), channel_id=1, source_target_pairs={{0,160},{32,192},{64,224},{96,0},{128,32},{160,64},{192,96},{224,1... | collective-permute-start | bytes 393224 | tf_op jit(solution)/shard_map/ppermute | solution.py:263
  167.9 21.4 %collective-permute-start.17 = (bf16[256,256]{1,0:T(8,128)(2,1)S(1)}, bf16[256,256]{1,0:T(8,128)(2,1)S(1)}, u32[]{:S(2)}, u32[]{:S(2)}) collective-permute-start(bf16[256,256]{1,0:T(8,128)(2,1)S(1)} %get-tuple-element.72), channel_id=1, source_target_pairs={{0,64},{32,96},{64,128},{96,160},{128,192},{160,224},{192,0},{224,... | collective-permute-start | bytes 393224 | tf_op jit(solution)/shard_map/ppermute | solution.py:263
  171.9 18.0 %collective-permute-start.18 = (bf16[256,256]{1,0:T(8,128)(2,1)S(1)}, bf16[256,256]{1,0:T(8,128)(2,1)S(1)}, u32[]{:S(2)}, u32[]{:S(2)}) collective-permute-start(bf16[256,256]{1,0:T(8,128)(2,1)S(1)} %get-tuple-element.71), channel_id=1, source_target_pairs={{0,192},{32,224},{64,0},{96,32},{128,64},{160,96},{192,128},{224,1... | collective-permute-start | bytes 393224 | tf_op jit(solution)/shard_map/ppermute | solution.py:263
  174.8 21.1 %collective-permute-start.28 = (bf16[384,256]{1,0:T(8,128)(2,1)S(1)}, bf16[384,256]{1,0:T(8,128)(2,1)S(1)}, u32[]{:S(2)}, u32[]{:S(2)}) collective-permute-start(bf16[384,256]{1,0:T(8,128)(2,1)S(1)} %add_convert_fusion.4), channel_id=1, source_target_pairs={{0,8},{8,16},{16,24},{24,0},{1,9},{9,17},{17,25},{25,1},{2,10},{10... | collective-permute-start | bytes 589832 | tf_op jit(solution)/shard_map/ppermute | solution.py:263
  187.4 8.5 %collective-permute-start.29 = (bf16[384,256]{1,0:T(8,128)(2,1)S(1)}, bf16[384,256]{1,0:T(8,128)(2,1)S(1)}, u32[]{:S(2)}, u32[]{:S(2)}) collective-permute-start(bf16[384,256]{1,0:T(8,128)(2,1)S(1)} %add_convert_fusion.4), channel_id=1, source_target_pairs={{0,16},{8,24},{16,0},{24,8},{1,17},{9,25},{17,1},{25,9},{2,18},{10... | collective-permute-start | bytes 589832 | tf_op jit(solution)/shard_map/ppermute | solution.py:263
  187.5 8.8 %collective-permute-start.30 = (bf16[384,256]{1,0:T(8,128)(2,1)S(1)}, bf16[384,256]{1,0:T(8,128)(2,1)S(1)}, u32[]{:S(2)}, u32[]{:S(2)}) collective-permute-start(bf16[384,256]{1,0:T(8,128)(2,1)S(1)} %add_convert_fusion.4), channel_id=1, source_target_pairs={{0,24},{8,0},{16,8},{24,16},{1,25},{9,1},{17,9},{25,17},{2,26},{10... | collective-permute-start | bytes 589832 | tf_op jit(solution)/shard_map/ppermute | solution.py:263
  189.4 5.3 %collective-permute-start.19 = (bf16[256,256]{1,0:T(8,128)(2,1)S(1)}, bf16[256,256]{1,0:T(8,128)(2,1)S(1)}, u32[]{:S(2)}, u32[]{:S(2)}) collective-permute-start(bf16[256,256]{1,0:T(8,128)(2,1)S(1)} %get-tuple-element.70), channel_id=1, source_target_pairs={{0,32},{32,64},{64,96},{96,128},{128,160},{160,192},{192,224},{224... | collective-permute-start | bytes 393224 | tf_op jit(solution)/shard_map/ppermute | solution.py:263
  189.9 4.8 %collective-permute-start.20 = (bf16[256,256]{1,0:T(8,128)(2,1)S(1)}, bf16[256,256]{1,0:T(8,128)(2,1)S(1)}, u32[]{:S(2)}, u32[]{:S(2)}) collective-permute-start(bf16[256,256]{1,0:T(8,128)(2,1)S(1)} %get-tuple-element.69), channel_id=1, source_target_pairs={{0,224},{32,0},{64,32},{96,64},{128,96},{160,128},{192,160},{224,1... | collective-permute-start | bytes 393224 | tf_op jit(solution)/shard_map/ppermute | solution.py:263
  196.7 3.6 %collective-permute-start.31 = (bf16[6,256,256]{2,1,0:T(8,128)(2,1)S(1)}, bf16[6,256,256]{2,1,0:T(8,128)(2,1)S(1)}, u32[]{:S(2)}, u32[]{:S(2)}) collective-permute-start(bf16[6,256,256]{2,1,0:T(8,128)(2,1)S(1)} %bitcast.116), channel_id=1, source_target_pairs={{0,4},{4,0},{1,5},{5,1},{2,6},{6,2},{3,7},{7,3},{8,12},{12,8},{9,1... | collective-permute-start | bytes 2359304 | tf_op jit(solution)/shard_map/ppermute | solution.py:263
  (13 other events, 192.5 us)

commit v3 on v2

--- a/solution.py
+++ b/solution.py
@@ -9,7 +9,7 @@
 
 BF = jnp.bfloat16
 F32 = jnp.float32
-Z_ORDER = (4, 3, -3, 2, -2, 1, -1, 0)
+Z_ORDER = (4, -3, 3, -2, 2, -1, 1, 0)
 Z_BUNDLES = (8,)
 
 
@@ -370,7 +370,7 @@
         dx == 0, 0, jnp.where(dx == 3, 1, jnp.where(dx == 1, 2, 3 + upper))
     ) + 5 * other_core
     bank_row = 2 * (owner_z - jnp.where(dx == 2, upper * (z_size // 2), 0)) + block
-    position = jnp.where(dz == 0, 7, jnp.where(dz == 4, 0, jnp.where(dz < 4, 7 - 2 * dz, 2 * dz - 8)))
+    position = jnp.where(dz == 0, 7, jnp.where(dz == 4, 0, jnp.where(dz < 4, 8 - 2 * dz, 2 * dz - 9)))
     place = 2 * (dx * z_size + position) + block
     place = place + 2 * x_size * z_size * other_core
     where = jnp.stack([bank, bank_row, place]).astype(jnp.int32)

time: 203 us -> 203 us (level)
  starting transfers between devices: 42.6 us -> 37.7 us
  waiting for transfers between devices: 65.9 us -> 70.6 us
    ppermute x29, starting transfers between devices: 39.6 us -> 34.6 us  [shift(): lax.ppermute(values, axis, [(i, (i + by) % size) for i in range(size)])]
    ppermute x29, waiting for transfers between devices: 49.8 us -> 52.7 us  [shift(): lax.ppermute(values, axis, [(i, (i + by) % size) for i in range(size)])]
  transfers between devices with their start and end apart: 32 -> 32, of which waited for: 16 -> 18; matrix products, arithmetic and copies ran while one was open for 8% -> 8% of each run, Pallas kernels for 6% -> 6%
where the time goes in v3:
time: 203 us; the launch traced here: 202 us
  waiting for transfers between devices  70.6 us (35%)
  starting transfers between devices  37.7 us (19%)
  blocking collectives  36.1 us (18%)
  Pallas kernels  27.7 us (14%)
  other arithmetic  16 us (8%)
  matrix products  6.78 us (3%)
  local copies, waits for them, and re-layouts  5.01 us (2%)
  between operations  2.27 us (1%)
    ppermute x29, waiting for transfers between devices, shift(): lax.ppermute(values, axis, [(i, (i + by) % size) for i in range(size)])  52.7 us
    all_to_all x1, blocking collectives, exchange(): return lax.all_to_all(values, axis, 0, 0, tiled=True)  36.1 us
    ppermute x29, starting transfers between devices, shift(): lax.ppermute(values, axis, [(i, (i + by) % size) for i in range(size)])  34.6 us
    ppermute x3, waiting for transfers between devices, pair(): return lax.ppermute(values, axis, [(i, i ^ bit) for i in range(size)])  17.9 us
    pallas_call x1, Pallas kernels, score(): pl.pallas_call(lambda *refs: score_kernel(*refs, per_group=per_group, ban...  16.2 us
    pallas_call x1, Pallas kernels, make_queries(): pl.pallas_call(lambda *refs: query_kernel(*refs, groups=groups), out_shap...  6.73 us
    pallas_call x1, Pallas kernels, head_product(): pl.pallas_call(head_kernel, out_shape=(half, half, jax.ShapeDtypeStruct((...  4.76 us
  transfers between devices with their start and end apart: 32, of which 18 were waited for; matrix products, arithmetic and copies ran while one was open for 8% of the time, Pallas kernels for 6%

profile of v3, /device:TPU:1, one launch (start us, length us, event | category | flops | bytes accessed | tf_op | source)
XLA Modules:
  0.0 202.1 jit_solution(17351269462482531166)
XLA Ops:
  1.9 3.1 %fusion.5 = bf16[1024,256]{1,0:T(8,128)(2,1)S(1)} fusion(bf16[1024,5]{1,0:T(8,128)(2,1)S(1)} %reshape_reshape.3, bf16[5,256]{1,0:T(8,128)(2,1)} %param.9), kind=kOutput, calls=%fused_computation.12 | convolution fusion | flops 19660800 | bytes 537088 | tf_op jit(solution)/shard_map/dot_general | solution.py:24
  7.7 36.1 %all_to_all.5 = bf16[8,256,256]{2,1,0:T(8,128)(2,1)S(1)} all-to-all(bf16[8,256,256]{2,1,0:T(8,128)(2,1)S(1)} %broadcast_in_dim.14), channel_id=1, replica_groups=mesh['z'=8,'x'=4,'c'=2,'rep'=4] {'z'}, dimensions={0} | all-to-all | bytes 2097152 | tf_op jit(solution)/shard_map/all_to_all | solution.py:267
  48.6 6.7 %queries.1 = (bf16[8,384,256]{2,1,0:T(8,128)(2,1)}, bf16[8,384,256]{2,1,0:T(8,128)(2,1)}, f32[8,384,3]{2,1,0:T(8,128)}) custom-call(bf16[256,256]{1,0:T(8,128)(2,1)} %copy-done.4, bf16[256,256]{1,0:T(8,128)(2,1)} %fusion.38.refs_1_.ctx_ref, bf16[12,256,256]{2,1,0:T(8,128)(2,1)} %bitcast.120), custom_call_target="tpu_custom_call" | custom-call | tf_op jit(solution)/shard_map/queries/pallas_call | solution.py:195
  55.3 11.8 %collective-permute-done = bf16[8,256,256]{2,1,0:T(8,128)(2,1)S(1)} collective-permute-done((bf16[8,256,256]{2,1,0:T(8,128)(2,1)S(1)}, bf16[8,256,256]{2,1,0:T(8,128)(2,1)S(1)}, u32[]{:S(2)}, u32[]{:S(2)}) %collective-permute-start) | collective-permute-done | bytes 1048608 | tf_op jit(solution)/shard_map/ppermute | solution.py:263
  69.8 1.7 collective-permute-start.3
  71.6 3.9 %collective-permute-start.4 = (bf16[8,256,256]{2,1,0:T(8,128)(2,1)S(1)}, bf16[8,256,256]{2,1,0:T(8,128)(2,1)}, u32[]{:S(2)}, u32[]{:S(2)}) collective-permute-start(bf16[8,256,256]{2,1,0:T(8,128)(2,1)S(1)} %all_to_all.5), channel_id=1, source_target_pairs={{0,4},{4,0},{1,5},{5,1},{2,6},{6,2},{3,7},{7,3},{8,12},{12,8},{9,1... | collective-permute-start | bytes 3145736 | tf_op jit(solution)/shard_map/ppermute | solution.py:263
  76.3 3.3 %collective-permute-done.2 = bf16[4,256,256]{2,1,0:T(8,128)(2,1)} collective-permute-done((bf16[4,256,256]{2,1,0:T(8,128)(2,1)}, bf16[4,256,256]{2,1,0:T(8,128)(2,1)}, u32[]{:S(2)}, u32[]{:S(2)}) %collective-permute-start.2) | collective-permute-done | bytes 524320 | tf_op jit(solution)/shard_map/ppermute | solution.py:263
  79.6 4.3 %collective-permute-start.7 = (bf16[4,256,256]{2,1,0:T(8,128)(2,1)}, bf16[4,256,256]{2,1,0:T(8,128)(2,1)S(1)}, u32[]{:S(2)}, u32[]{:S(2)}) collective-permute-start(bf16[4,256,256]{2,1,0:T(8,128)(2,1)} %collective-permute-done.2), channel_id=1, source_target_pairs={{0,4},{4,0},{1,5},{5,1},{2,6},{6,2},{3,7},{7,3},{8,12},{12,8},{9,1... | collective-permute-start | bytes 1572872 | tf_op jit(solution)/shard_map/ppermute | solution.py:263
  87.2 16.2 %score.1 = (bf16[64,128,256]{2,1,0:T(8,128)(2,1)}, bf16[64,128,256]{2,1,0:T(8,128)(2,1)}, bf16[12,256,256]{2,1,0:T(8,128)(2,1)}, bf16[12,256,256]{2,1,0:T(8,128)(2,1)}) custom-call(s32[3,32]{1,0:T(4,128)} %pad_add_fusion.refs_0_, bf16[8,384,256]{2,1,0:T(8,128)(2,1)} %get-tuple-element.32.refs_1_, bf16[8,384,256]{2,1,0:T(8,128)(2,1)} %get-tuple-element.33.refs_2_, ...), custom_call_target="tpu_custom_call" | custom-call | tf_op jit(solution)/shard_map/score/pallas_call | solution.py:220
  103.9 4.8 %heads.1 = (bf16[6,256,256]{2,1,0:T(8,128)(2,1)}, bf16[6,256,256]{2,1,0:T(8,128)(2,1)}, f32[256,256]{1,0:T(8,128)}) custom-call(s32[1]{0:T(128)} %bitcast.core_ref, bf16[256,256]{1,0:T(8,128)(2,1)} %fusion.38.refs_1_.ctx_ref, bf16[12,256,256]{2,1,0:T(8,128)(2,1)} %get-tuple-element.37.pg_ref, bf16[12,256,256]{2,1,0:T(8,128)(2,1)} %get-tuple-element.38.p_ref), custom_call_target="tpu_custom_call" | custom-call | tf_op jit(solution)/shard_map/heads/pallas_call | solution.py:251
  108.8 2.2 %collective-permute-done.9 = bf16[4,8,256,256]{3,2,1,0:T(8,128)(2,1)} collective-permute-done((bf16[4,8,256,256]{3,2,1,0:T(8,128)(2,1)}, bf16[4,8,256,256]{3,2,1,0:T(8,128)(2,1)}, u32[]{:S(2)}, u32[]{:S(2)}) %collective-permute-start.9) | collective-permute-done | bytes 4194336 | tf_op jit(solution)/shard_map/ppermute | solution.py:263
  111.1 2.7 %fusion.17 = (bf16[8,128,256]{2,1,0:T(8,128)(2,1)S(1)}, bf16[8,128,256]{2,1,0:T(8,128)(2,1)}) fusion(bf16[4,8,256,256]{3,2,1,0:T(8,128)(2,1)} %collective-permute-done.9, bf16[4,8,256,256]{3,2,1,0:T(8,128)(2,1)} %bitcast.109), kind=kLoop, calls=%fused_computation.38 | loop fusion | flops 2097152 | bytes 3145728 | tf_op jit(solution)/shard_map/convert_element_type | solution.py:320
  114.5 2.0 %collective-permute-start.11 = (bf16[8,128,256]{2,1,0:T(8,128)(2,1)S(1)}, bf16[8,128,256]{2,1,0:T(8,128)(2,1)S(1)}, u32[]{:S(2)}, u32[]{:S(2)}) collective-permute-start(bf16[8,128,256]{2,1,0:T(8,128)(2,1)S(1)} %get-tuple-element.65), channel_id=1, source_target_pairs={{0,24},{8,0},{16,8},{24,16},{1,25},{9,1},{17,9},{25,17},{2,26},{10... | collective-permute-start | bytes 1572872 | tf_op jit(solution)/shard_map/ppermute | solution.py:263
  116.8 2.7 %collective-permute-start.23 = (bf16[384,256]{1,0:T(8,128)(2,1)S(1)}, bf16[384,256]{1,0:T(8,128)(2,1)S(1)}, u32[]{:S(2)}, u32[]{:S(2)}) collective-permute-start(bf16[384,256]{1,0:T(8,128)(2,1)S(1)} %get-tuple-element.82), channel_id=1, source_target_pairs={{0,24},{8,0},{16,8},{24,16},{1,25},{9,1},{17,9},{25,17},{2,26},{10... | collective-permute-start | bytes 589832 | tf_op jit(solution)/shard_map/ppermute | solution.py:263
  119.5 9.0 %collective-permute-done.10 = bf16[8,128,256]{2,1,0:T(8,128)(2,1)S(1)} collective-permute-done((bf16[8,128,256]{2,1,0:T(8,128)(2,1)}, bf16[8,128,256]{2,1,0:T(8,128)(2,1)S(1)}, u32[]{:S(2)}, u32[]{:S(2)}) %collective-permute-start.10) | collective-permute-done | bytes 524320 | tf_op jit(solution)/shard_map/ppermute | solution.py:263
  128.5 3.9 %fusion.1 = (bf16[8,256,256]{2,1,0:T(8,128)(2,1)S(1)}, bf16[8,256,256]{2,1,0:T(8,128)(2,1)}) fusion(bf16[8,128,256]{2,1,0:T(8,128)(2,1)S(1)} %collective-permute-done.10, bf16[4,8,256,256]{3,2,1,0:T(8,128)(2,1)} %collective-permute-done.9, bf16[4,8,256,256]{3,2,1,0:T(8,128)(2,1)} %bitcast.110, bf16[8,128,256]{2,1,0:T(8,128)(2,1)S(1)} %collective-permute-done.11), kind=kLoop, calls=%fused_computation.4 | loop fusion | flops 6291456 | bytes 7340032 | tf_op jit(solution)/shard_map/convert_element_type | solution.py:328
  132.4 2.1 %collective-permute-start.13 = (bf16[8,256,256]{2,1,0:T(8,128)(2,1)}, bf16[8,256,256]{2,1,0:T(8,128)(2,1)S(1)}, u32[]{:S(2)}, u32[]{:S(2)}) collective-permute-start(bf16[8,256,256]{2,1,0:T(8,128)(2,1)} %get-tuple-element.64), channel_id=1, source_target_pairs={{0,24},{8,0},{16,8},{24,16},{1,25},{9,1},{17,9},{25,17},{2,26},{10... | collective-permute-start | bytes 3145736 | tf_op jit(solution)/shard_map/ppermute | solution.py:263
  134.6 3.4 %collective-permute-done.24 = bf16[384,256]{1,0:T(8,128)(2,1)S(1)} collective-permute-done((bf16[384,256]{1,0:T(8,128)(2,1)S(1)}, bf16[384,256]{1,0:T(8,128)(2,1)S(1)}, u32[]{:S(2)}, u32[]{:S(2)}) %collective-permute-start.24) | collective-permute-done | bytes 196640 | tf_op jit(solution)/shard_map/ppermute | solution.py:263
  138.2 4.8 %collective-permute-done.25 = bf16[384,256]{1,0:T(8,128)(2,1)S(1)} collective-permute-done((bf16[384,256]{1,0:T(8,128)(2,1)S(1)}, bf16[384,256]{1,0:T(8,128)(2,1)S(1)}, u32[]{:S(2)}, u32[]{:S(2)}) %collective-permute-start.25) | collective-permute-done | bytes 196640 | tf_op jit(solution)/shard_map/ppermute | solution.py:291
  143.9 10.8 %collective-permute-done.26 = bf16[384,256]{1,0:T(8,128)(2,1)} collective-permute-done((bf16[384,256]{1,0:T(8,128)(2,1)}, bf16[384,256]{1,0:T(8,128)(2,1)}, u32[]{:S(2)}, u32[]{:S(2)}) %collective-permute-start.26) | collective-permute-done | bytes 196640 | tf_op jit(solution)/shard_map/ppermute | solution.py:291
  155.8 2.8 %collective-permute-start.27 = (bf16[384,256]{1,0:T(8,128)(2,1)S(1)}, bf16[384,256]{1,0:T(8,128)(2,1)S(1)}, u32[]{:S(2)}, u32[]{:S(2)}) collective-permute-start(bf16[384,256]{1,0:T(8,128)(2,1)S(1)} %add_convert_fusion.6), channel_id=1, source_target_pairs={{0,128},{32,160},{64,192},{96,224},{128,0},{160,32},{192,64},{224,... | collective-permute-start | bytes 589832 | tf_op jit(solution)/shard_map/ppermute | solution.py:291
  158.8 2.1 %fusion.94 = (bf16[8,256,256]{2,1,0:T(8,128)(2,1)S(1)}, f32[8,256,256]{2,1,0:T(8,128)S(1)}) fusion(bf16[8,256,256]{2,1,0:T(8,128)(2,1)S(1)} %collective-permute-done.13, bf16[8,256,256]{2,1,0:T(8,128)(2,1)S(1)} %collective-permute-done.12, bf16[4,8,256,256]{3,2,1,0:T(8,128)(2,1)} %collective-permute-done.9, bf16[4,8,256,256]{3,2,1,0:T(8,128)(2,1)} %bitcast.111), kind=kLoop, calls=%fused_computation.192 | loop fusion | flops 4194304 | bytes 7340032 | tf_op jit(solution)/shard_map/convert.7
  160.9 2.5 %collective-permute-start.14 = (bf16[256,256]{1,0:T(8,128)(2,1)S(1)}, bf16[256,256]{1,0:T(8,128)(2,1)S(1)}, u32[]{:S(2)}, u32[]{:S(2)}) collective-permute-start(bf16[256,256]{1,0:T(8,128)(2,1)S(1)} %get-tuple-element.75), channel_id=1, source_target_pairs={{0,128},{32,160},{64,192},{96,224},{128,0},{160,32},{192,64},{224,... | collective-permute-start | bytes 393224 | tf_op jit(solution)/shard_map/ppermute | solution.py:263
  164.4 2.4 %collective-permute-start.16 = (bf16[256,256]{1,0:T(8,128)(2,1)S(1)}, bf16[256,256]{1,0:T(8,128)(2,1)S(1)}, u32[]{:S(2)}, u32[]{:S(2)}) collective-permute-start(bf16[256,256]{1,0:T(8,128)(2,1)S(1)} %get-tuple-element.73), channel_id=1, source_target_pairs={{0,96},{32,128},{64,160},{96,192},{128,224},{160,0},{192,32},{224,... | collective-permute-start | bytes 393224 | tf_op jit(solution)/shard_map/ppermute | solution.py:263
  166.7 1.5 collective-permute-start.17
  169.4 2.3 %collective-permute-done.27 = bf16[384,256]{1,0:T(8,128)(2,1)S(1)} collective-permute-done((bf16[384,256]{1,0:T(8,128)(2,1)S(1)}, bf16[384,256]{1,0:T(8,128)(2,1)S(1)}, u32[]{:S(2)}, u32[]{:S(2)}) %collective-permute-start.27) | collective-permute-done | bytes 196640 | tf_op jit(solution)/shard_map/ppermute | solution.py:291
  171.8 3.0 %collective-permute-done.14 = bf16[256,256]{1,0:T(8,128)(2,1)S(1)} collective-permute-done((bf16[256,256]{1,0:T(8,128)(2,1)S(1)}, bf16[256,256]{1,0:T(8,128)(2,1)S(1)}, u32[]{:S(2)}, u32[]{:S(2)}) %collective-permute-start.14) | collective-permute-done | bytes 131104 | tf_op jit(solution)/shard_map/ppermute | solution.py:263
  174.8 7.4 %collective-permute-done.15 = bf16[256,256]{1,0:T(8,128)(2,1)S(1)} collective-permute-done((bf16[256,256]{1,0:T(8,128)(2,1)S(1)}, bf16[256,256]{1,0:T(8,128)(2,1)S(1)}, u32[]{:S(2)}, u32[]{:S(2)}) %collective-permute-start.15) | collective-permute-done | bytes 131104 | tf_op jit(solution)/shard_map/ppermute | solution.py:263
  182.2 5.1 %collective-permute-done.16 = bf16[256,256]{1,0:T(8,128)(2,1)S(1)} collective-permute-done((bf16[256,256]{1,0:T(8,128)(2,1)S(1)}, bf16[256,256]{1,0:T(8,128)(2,1)S(1)}, u32[]{:S(2)}, u32[]{:S(2)}) %collective-permute-start.16) | collective-permute-done | bytes 131104 | tf_op jit(solution)/shard_map/ppermute | solution.py:263
  190.1 3.0 %collective-permute-done.19 = bf16[256,256]{1,0:T(8,128)(2,1)S(1)} collective-permute-done((bf16[256,256]{1,0:T(8,128)(2,1)S(1)}, bf16[256,256]{1,0:T(8,128)(2,1)S(1)}, u32[]{:S(2)}, u32[]{:S(2)}) %collective-permute-start.19) | collective-permute-done | bytes 131104 | tf_op jit(solution)/shard_map/ppermute | solution.py:263
  195.2 2.9 %collective-permute-start.31 = (bf16[6,256,256]{2,1,0:T(8,128)(2,1)S(1)}, bf16[6,256,256]{2,1,0:T(8,128)(2,1)S(1)}, u32[]{:S(2)}, u32[]{:S(2)}) collective-permute-start(bf16[6,256,256]{2,1,0:T(8,128)(2,1)S(1)} %bitcast.116), channel_id=1, source_target_pairs={{0,4},{4,0},{1,5},{5,1},{2,6},{6,2},{3,7},{7,3},{8,12},{12,8},{9,1... | collective-permute-start | bytes 2359304 | tf_op jit(solution)/shard_map/ppermute | solution.py:263
  200.1 2.0 convert_multiply_fusion
  (108 shorter events, 27.3 us)
Async XLA Ops:
  43.7 23.4 %collective-permute-start = (bf16[8,256,256]{2,1,0:T(8,128)(2,1)S(1)}, bf16[8,256,256]{2,1,0:T(8,128)(2,1)S(1)}, u32[]{:S(2)}, u32[]{:S(2)}) collective-permute-start(bf16[8,256,256]{2,1,0:T(8,128)(2,1)S(1)} %all_to_all.5), channel_id=1, source_target_pairs={{0,8},{8,16},{16,24},{24,0},{1,9},{9,17},{17,25},{25,1},{2,10},{10... | collective-permute-start | bytes 3145736 | tf_op jit(solution)/shard_map/ppermute | solution.py:263
  44.9 22.2 %collective-permute-start.1 = (bf16[8,256,256]{2,1,0:T(8,128)(2,1)S(1)}, bf16[8,256,256]{2,1,0:T(8,128)(2,1)S(1)}, u32[]{:S(2)}, u32[]{:S(2)}) collective-permute-start(bf16[8,256,256]{2,1,0:T(8,128)(2,1)S(1)} %all_to_all.5), channel_id=1, source_target_pairs={{0,24},{8,0},{16,8},{24,16},{1,25},{9,1},{17,9},{25,17},{2,26},{10... | collective-permute-start | bytes 3145736 | tf_op jit(solution)/shard_map/ppermute | solution.py:263
  68.1 11.6 %collective-permute-start.2 = (bf16[4,256,256]{2,1,0:T(8,128)(2,1)}, bf16[4,256,256]{2,1,0:T(8,128)(2,1)}, u32[]{:S(2)}, u32[]{:S(2)}) collective-permute-start(bf16[4,256,256]{2,1,0:T(8,128)(2,1)} %slice.97), channel_id=1, source_target_pairs={{0,8},{8,16},{16,24},{24,0},{1,9},{9,17},{17,25},{25,1},{2,10},{10... | collective-permute-start | bytes 1572872 | tf_op jit(solution)/shard_map/ppermute | solution.py:263
  69.8 14.1 %collective-permute-start.3 = (bf16[4,256,256]{2,1,0:T(8,128)(2,1)}, bf16[4,256,256]{2,1,0:T(8,128)(2,1)}, u32[]{:S(2)}, u32[]{:S(2)}) collective-permute-start(bf16[4,256,256]{2,1,0:T(8,128)(2,1)} %slice.98), channel_id=1, source_target_pairs={{0,24},{8,0},{16,8},{24,16},{1,25},{9,1},{17,9},{25,17},{2,26},{10... | collective-permute-start | bytes 1572872 | tf_op jit(solution)/shard_map/ppermute | solution.py:263
  71.6 13.5 %collective-permute-start.4 = (bf16[8,256,256]{2,1,0:T(8,128)(2,1)S(1)}, bf16[8,256,256]{2,1,0:T(8,128)(2,1)}, u32[]{:S(2)}, u32[]{:S(2)}) collective-permute-start(bf16[8,256,256]{2,1,0:T(8,128)(2,1)S(1)} %all_to_all.5), channel_id=1, source_target_pairs={{0,4},{4,0},{1,5},{5,1},{2,6},{6,2},{3,7},{7,3},{8,12},{12,8},{9,1... | collective-permute-start | bytes 3145736 | tf_op jit(solution)/shard_map/ppermute | solution.py:263
  75.5 10.9 %collective-permute-start.5 = (bf16[8,256,256]{2,1,0:T(8,128)(2,1)S(1)}, bf16[8,256,256]{2,1,0:T(8,128)(2,1)}, u32[]{:S(2)}, u32[]{:S(2)}) collective-permute-start(bf16[8,256,256]{2,1,0:T(8,128)(2,1)S(1)} %collective-permute-done), channel_id=1, source_target_pairs={{0,4},{4,0},{1,5},{5,1},{2,6},{6,2},{3,7},{7,3},{8,12},{12,8},{9,1... | collective-permute-start | bytes 3145736 | tf_op jit(solution)/shard_map/ppermute | solution.py:263
  75.5 10.9 %collective-permute-start.6 = (bf16[8,256,256]{2,1,0:T(8,128)(2,1)S(1)}, bf16[8,256,256]{2,1,0:T(8,128)(2,1)}, u32[]{:S(2)}, u32[]{:S(2)}) collective-permute-start(bf16[8,256,256]{2,1,0:T(8,128)(2,1)S(1)} %collective-permute-done.1), channel_id=1, source_target_pairs={{0,4},{4,0},{1,5},{5,1},{2,6},{6,2},{3,7},{7,3},{8,12},{12,8},{9,1... | collective-permute-start | bytes 3145736 | tf_op jit(solution)/shard_map/ppermute | solution.py:263
  79.6 6.0 %collective-permute-start.7 = (bf16[4,256,256]{2,1,0:T(8,128)(2,1)}, bf16[4,256,256]{2,1,0:T(8,128)(2,1)S(1)}, u32[]{:S(2)}, u32[]{:S(2)}) collective-permute-start(bf16[4,256,256]{2,1,0:T(8,128)(2,1)} %collective-permute-done.2), channel_id=1, source_target_pairs={{0,4},{4,0},{1,5},{5,1},{2,6},{6,2},{3,7},{7,3},{8,12},{12,8},{9,1... | collective-permute-start | bytes 1572872 | tf_op jit(solution)/shard_map/ppermute | solution.py:263
  83.9 2.5 %collective-permute-start.8 = (bf16[4,256,256]{2,1,0:T(8,128)(2,1)}, bf16[4,256,256]{2,1,0:T(8,128)(2,1)S(1)}, u32[]{:S(2)}, u32[]{:S(2)}) collective-permute-start(bf16[4,256,256]{2,1,0:T(8,128)(2,1)} %collective-permute-done.3), channel_id=1, source_target_pairs={{0,4},{4,0},{1,5},{5,1},{2,6},{6,2},{3,7},{7,3},{8,12},{12,8},{9,1... | collective-permute-start | bytes 1572872 | tf_op jit(solution)/shard_map/ppermute | solution.py:263
  103.5 7.6 %collective-permute-start.9 = (bf16[4,8,256,256]{3,2,1,0:T(8,128)(2,1)}, bf16[4,8,256,256]{3,2,1,0:T(8,128)(2,1)}, u32[]{:S(2)}, u32[]{:S(2)}) collective-permute-start(bf16[4,8,256,256]{3,2,1,0:T(8,128)(2,1)} %bitcast.128), channel_id=1, source_target_pairs={{0,4},{4,0},{1,5},{5,1},{2,6},{6,2},{3,7},{7,3},{8,12},{12,8},{9,1... | collective-permute-start | bytes 12582920 | tf_op jit(solution)/shard_map/ppermute | solution.py:263
  108.7 7.8 %collective-permute-start.21 = (bf16[6,256,256]{2,1,0:T(8,128)(2,1)}, bf16[6,256,256]{2,1,0:T(8,128)(2,1)S(1)}, u32[]{:S(2)}, u32[]{:S(2)}) collective-permute-start(bf16[6,256,256]{2,1,0:T(8,128)(2,1)} %get-tuple-element.55), channel_id=1, source_target_pairs={{0,4},{4,0},{1,5},{5,1},{2,6},{6,2},{3,7},{7,3},{8,12},{12,8},{9,1... | collective-permute-start | bytes 2359304 | tf_op jit(solution)/shard_map/ppermute | solution.py:263
  113.7 14.7 %collective-permute-start.10 = (bf16[8,128,256]{2,1,0:T(8,128)(2,1)}, bf16[8,128,256]{2,1,0:T(8,128)(2,1)S(1)}, u32[]{:S(2)}, u32[]{:S(2)}) collective-permute-start(bf16[8,128,256]{2,1,0:T(8,128)(2,1)} %get-tuple-element.66), channel_id=1, source_target_pairs={{0,8},{8,16},{16,24},{24,0},{1,9},{9,17},{17,25},{25,1},{2,10},{10... | collective-permute-start | bytes 1572872 | tf_op jit(solution)/shard_map/ppermute | solution.py:263
  114.5 14.0 %collective-permute-start.11 = (bf16[8,128,256]{2,1,0:T(8,128)(2,1)S(1)}, bf16[8,128,256]{2,1,0:T(8,128)(2,1)S(1)}, u32[]{:S(2)}, u32[]{:S(2)}) collective-permute-start(bf16[8,128,256]{2,1,0:T(8,128)(2,1)S(1)} %get-tuple-element.65), channel_id=1, source_target_pairs={{0,24},{8,0},{16,8},{24,16},{1,25},{9,1},{17,9},{25,17},{2,26},{10... | collective-permute-start | bytes 1572872 | tf_op jit(solution)/shard_map/ppermute | solution.py:263
  116.7 17.8 %collective-permute-start.22 = (bf16[384,256]{1,0:T(8,128)(2,1)S(1)}, bf16[384,256]{1,0:T(8,128)(2,1)S(1)}, u32[]{:S(2)}, u32[]{:S(2)}) collective-permute-start(bf16[384,256]{1,0:T(8,128)(2,1)S(1)} %get-tuple-element.80), channel_id=1, source_target_pairs={{0,8},{8,16},{16,24},{24,0},{1,9},{9,17},{17,25},{25,1},{2,10},{10... | collective-permute-start | bytes 589832 | tf_op jit(solution)/shard_map/ppermute | solution.py:263
  116.8 17.7 %collective-permute-start.23 = (bf16[384,256]{1,0:T(8,128)(2,1)S(1)}, bf16[384,256]{1,0:T(8,128)(2,1)S(1)}, u32[]{:S(2)}, u32[]{:S(2)}) collective-permute-start(bf16[384,256]{1,0:T(8,128)(2,1)S(1)} %get-tuple-element.82), channel_id=1, source_target_pairs={{0,24},{8,0},{16,8},{24,16},{1,25},{9,1},{17,9},{25,17},{2,26},{10... | collective-permute-start | bytes 589832 | tf_op jit(solution)/shard_map/ppermute | solution.py:263
  119.5 18.5 %collective-permute-start.24 = (bf16[384,256]{1,0:T(8,128)(2,1)S(1)}, bf16[384,256]{1,0:T(8,128)(2,1)S(1)}, u32[]{:S(2)}, u32[]{:S(2)}) collective-permute-start(bf16[384,256]{1,0:T(8,128)(2,1)S(1)} %get-tuple-element.81), channel_id=1, source_target_pairs={{0,16},{8,24},{16,0},{24,8},{1,17},{9,25},{17,1},{25,9},{2,18},{10... | collective-permute-start | bytes 589832 | tf_op jit(solution)/shard_map/ppermute | solution.py:263
  132.4 26.2 %collective-permute-start.13 = (bf16[8,256,256]{2,1,0:T(8,128)(2,1)}, bf16[8,256,256]{2,1,0:T(8,128)(2,1)S(1)}, u32[]{:S(2)}, u32[]{:S(2)}) collective-permute-start(bf16[8,256,256]{2,1,0:T(8,128)(2,1)} %get-tuple-element.64), channel_id=1, source_target_pairs={{0,24},{8,0},{16,8},{24,16},{1,25},{9,1},{17,9},{25,17},{2,26},{10... | collective-permute-start | bytes 3145736 | tf_op jit(solution)/shard_map/ppermute | solution.py:263
  134.5 24.3 %collective-permute-start.12 = (bf16[8,256,256]{2,1,0:T(8,128)(2,1)S(1)}, bf16[8,256,256]{2,1,0:T(8,128)(2,1)S(1)}, u32[]{:S(2)}, u32[]{:S(2)}) collective-permute-start(bf16[8,256,256]{2,1,0:T(8,128)(2,1)S(1)} %get-tuple-element.63), channel_id=1, source_target_pairs={{0,8},{8,16},{16,24},{24,0},{1,9},{9,17},{17,25},{25,1},{2,10},{10... | collective-permute-start | bytes 3145736 | tf_op jit(solution)/shard_map/ppermute | solution.py:263
  138.1 4.9 %collective-permute-start.25 = (bf16[384,256]{1,0:T(8,128)(2,1)S(1)}, bf16[384,256]{1,0:T(8,128)(2,1)S(1)}, u32[]{:S(2)}, u32[]{:S(2)}) collective-permute-start(bf16[384,256]{1,0:T(8,128)(2,1)S(1)} %fusion.29), channel_id=1, source_target_pairs={{0,32},{32,0},{64,96},{96,64},{128,160},{160,128},{192,224},{224,1... | collective-permute-start | bytes 589832 | tf_op jit(solution)/shard_map/ppermute | solution.py:291
  143.7 11.0 %collective-permute-start.26 = (bf16[384,256]{1,0:T(8,128)(2,1)}, bf16[384,256]{1,0:T(8,128)(2,1)}, u32[]{:S(2)}, u32[]{:S(2)}) collective-permute-start(bf16[384,256]{1,0:T(8,128)(2,1)} %add_convert_fusion.7), channel_id=1, source_target_pairs={{0,64},{32,96},{64,0},{96,32},{128,192},{160,224},{192,128},{224,1... | collective-permute-start | bytes 589832 | tf_op jit(solution)/shard_map/ppermute | solution.py:291
  155.8 16.0 %collective-permute-start.27 = (bf16[384,256]{1,0:T(8,128)(2,1)S(1)}, bf16[384,256]{1,0:T(8,128)(2,1)S(1)}, u32[]{:S(2)}, u32[]{:S(2)}) collective-permute-start(bf16[384,256]{1,0:T(8,128)(2,1)S(1)} %add_convert_fusion.6), channel_id=1, source_target_pairs={{0,128},{32,160},{64,192},{96,224},{128,0},{160,32},{192,64},{224,... | collective-permute-start | bytes 589832 | tf_op jit(solution)/shard_map/ppermute | solution.py:291
  160.9 13.8 %collective-permute-start.14 = (bf16[256,256]{1,0:T(8,128)(2,1)S(1)}, bf16[256,256]{1,0:T(8,128)(2,1)S(1)}, u32[]{:S(2)}, u32[]{:S(2)}) collective-permute-start(bf16[256,256]{1,0:T(8,128)(2,1)S(1)} %get-tuple-element.75), channel_id=1, source_target_pairs={{0,128},{32,160},{64,192},{96,224},{128,0},{160,32},{192,64},{224,... | collective-permute-start | bytes 393224 | tf_op jit(solution)/shard_map/ppermute | solution.py:263
  163.5 18.7 %collective-permute-start.15 = (bf16[256,256]{1,0:T(8,128)(2,1)S(1)}, bf16[256,256]{1,0:T(8,128)(2,1)S(1)}, u32[]{:S(2)}, u32[]{:S(2)}) collective-permute-start(bf16[256,256]{1,0:T(8,128)(2,1)S(1)} %get-tuple-element.74), channel_id=1, source_target_pairs={{0,160},{32,192},{64,224},{96,0},{128,32},{160,64},{192,96},{224,1... | collective-permute-start | bytes 393224 | tf_op jit(solution)/shard_map/ppermute | solution.py:263
  164.4 23.0 %collective-permute-start.16 = (bf16[256,256]{1,0:T(8,128)(2,1)S(1)}, bf16[256,256]{1,0:T(8,128)(2,1)S(1)}, u32[]{:S(2)}, u32[]{:S(2)}) collective-permute-start(bf16[256,256]{1,0:T(8,128)(2,1)S(1)} %get-tuple-element.73), channel_id=1, source_target_pairs={{0,96},{32,128},{64,160},{96,192},{128,224},{160,0},{192,32},{224,... | collective-permute-start | bytes 393224 | tf_op jit(solution)/shard_map/ppermute | solution.py:263
  166.7 21.9 %collective-permute-start.17 = (bf16[256,256]{1,0:T(8,128)(2,1)S(1)}, bf16[256,256]{1,0:T(8,128)(2,1)S(1)}, u32[]{:S(2)}, u32[]{:S(2)}) collective-permute-start(bf16[256,256]{1,0:T(8,128)(2,1)S(1)} %get-tuple-element.72), channel_id=1, source_target_pairs={{0,192},{32,224},{64,0},{96,32},{128,64},{160,96},{192,128},{224,1... | collective-permute-start | bytes 393224 | tf_op jit(solution)/shard_map/ppermute | solution.py:263
  171.7 16.9 %collective-permute-start.18 = (bf16[256,256]{1,0:T(8,128)(2,1)S(1)}, bf16[256,256]{1,0:T(8,128)(2,1)S(1)}, u32[]{:S(2)}, u32[]{:S(2)}) collective-permute-start(bf16[256,256]{1,0:T(8,128)(2,1)S(1)} %get-tuple-element.71), channel_id=1, source_target_pairs={{0,64},{32,96},{64,128},{96,160},{128,192},{160,224},{192,0},{224,... | collective-permute-start | bytes 393224 | tf_op jit(solution)/shard_map/ppermute | solution.py:263
  174.8 20.1 %collective-permute-start.28 = (bf16[384,256]{1,0:T(8,128)(2,1)S(1)}, bf16[384,256]{1,0:T(8,128)(2,1)S(1)}, u32[]{:S(2)}, u32[]{:S(2)}) collective-permute-start(bf16[384,256]{1,0:T(8,128)(2,1)S(1)} %add_convert_fusion.4), channel_id=1, source_target_pairs={{0,8},{8,16},{16,24},{24,0},{1,9},{9,17},{17,25},{25,1},{2,10},{10... | collective-permute-start | bytes 589832 | tf_op jit(solution)/shard_map/ppermute | solution.py:263
  182.2 12.6 %collective-permute-start.29 = (bf16[384,256]{1,0:T(8,128)(2,1)S(1)}, bf16[384,256]{1,0:T(8,128)(2,1)S(1)}, u32[]{:S(2)}, u32[]{:S(2)}) collective-permute-start(bf16[384,256]{1,0:T(8,128)(2,1)S(1)} %add_convert_fusion.4), channel_id=1, source_target_pairs={{0,16},{8,24},{16,0},{24,8},{1,17},{9,25},{17,1},{25,9},{2,18},{10... | collective-permute-start | bytes 589832 | tf_op jit(solution)/shard_map/ppermute | solution.py:263
  187.3 7.5 %collective-permute-start.30 = (bf16[384,256]{1,0:T(8,128)(2,1)S(1)}, bf16[384,256]{1,0:T(8,128)(2,1)S(1)}, u32[]{:S(2)}, u32[]{:S(2)}) collective-permute-start(bf16[384,256]{1,0:T(8,128)(2,1)S(1)} %add_convert_fusion.4), channel_id=1, source_target_pairs={{0,24},{8,0},{16,8},{24,16},{1,25},{9,1},{17,9},{25,17},{2,26},{10... | collective-permute-start | bytes 589832 | tf_op jit(solution)/shard_map/ppermute | solution.py:263
  188.6 4.5 %collective-permute-start.19 = (bf16[256,256]{1,0:T(8,128)(2,1)S(1)}, bf16[256,256]{1,0:T(8,128)(2,1)S(1)}, u32[]{:S(2)}, u32[]{:S(2)}) collective-permute-start(bf16[256,256]{1,0:T(8,128)(2,1)S(1)} %get-tuple-element.70), channel_id=1, source_target_pairs={{0,224},{32,0},{64,32},{96,64},{128,96},{160,128},{192,160},{224,1... | collective-permute-start | bytes 393224 | tf_op jit(solution)/shard_map/ppermute | solution.py:263
  188.6 5.0 %collective-permute-start.20 = (bf16[256,256]{1,0:T(8,128)(2,1)S(1)}, bf16[256,256]{1,0:T(8,128)(2,1)S(1)}, u32[]{:S(2)}, u32[]{:S(2)}) collective-permute-start(bf16[256,256]{1,0:T(8,128)(2,1)S(1)} %get-tuple-element.69), channel_id=1, source_target_pairs={{0,32},{32,64},{64,96},{96,128},{128,160},{160,192},{192,224},{224... | collective-permute-start | bytes 393224 | tf_op jit(solution)/shard_map/ppermute | solution.py:263
  195.2 4.8 %collective-permute-start.31 = (bf16[6,256,256]{2,1,0:T(8,128)(2,1)S(1)}, bf16[6,256,256]{2,1,0:T(8,128)(2,1)S(1)}, u32[]{:S(2)}, u32[]{:S(2)}) collective-permute-start(bf16[6,256,256]{2,1,0:T(8,128)(2,1)S(1)} %bitcast.116), channel_id=1, source_target_pairs={{0,4},{4,0},{1,5},{5,1},{2,6},{6,2},{3,7},{7,3},{8,12},{12,8},{9,1... | collective-permute-start | bytes 2359304 | tf_op jit(solution)/shard_map/ppermute | solution.py:263
  (13 other events, 193.8 us)
